TPU v7x, 256 devices: a whole 4x4x8 slice. The times are simulated.
256 devices in a mesh: rows: 32 (over y, x, core), cols: 8 (over z).
Axes of the slice: x: 4, y: 4, z: 8, core: 2. Of those that a mesh axis runs over, the one named last changes fastest.
Arguments:
- tiles: float32 [32, 64, 128, 128], P('rows', 'cols'), may hold values from -0.1875 to 0.1875
- tile_rows: int32 [32, 64], P('rows', 'cols'), may hold values from 0 to 1
- tile_cols: int32 [32, 64], P('rows', 'cols'), may hold values from 0 to 15
- counts: int32 [32, 8], P('rows', 'cols'), may hold values from 1 to 8, as said below
- scaling: float32 [16384], P('cols'), may hold values from 0.1 to 10
Outputs:
- normal: float32 [8192, 8192], P('rows', 'cols')
Inputs may be any that keep to these rules, and one draw needn't show every extreme that they name: `counts`: in every draw some panels have all 8 slots live in every column group; the others have at most 5.
All inputs are finite; a program needn't handle non-finite values.
Results may differ from a plain program's by a relative error of at most 0.0003.
Values sent between devices are 32-bit elements; how exact they have to be, the bound alone decides.
A program may use at most 192 MiB of HBM per device.

v0:
```python
import jax
import jax.numpy as jnp
from jax import lax
from jax.sharding import PartitionSpec as P

TB = 128
RB = 2
CB_DEV = 16


def densify(tile_set, row_ids, col_ids, live_mask, scale_set, block_count):
    placed = jnp.zeros((block_count, RB, TB, TB), jnp.float32)
    placed = placed.at[col_ids, row_ids].add(tile_set * live_mask[:, None, None])
    placed = placed * scale_set[:, None, None, :]
    return placed.reshape(block_count, RB * TB, TB)


def place_panels(blocked, tile_set, row_ids, col_ids, live_mask, panel_count):
    picked = jnp.take(blocked, col_ids, axis=0)
    product = jnp.einsum("kac,kbc->kab", picked, tile_set, precision=lax.Precision.HIGHEST)
    product = product.reshape(panel_count, -1, RB * TB, TB)
    hit_row = (row_ids[:, None] == jnp.arange(RB, dtype=jnp.int32)[None, :]).astype(
        jnp.float32
    ) * live_mask[:, None]
    hit_row = hit_row.reshape(panel_count, -1, RB)
    placed = jnp.einsum("pkr,pkab->aprb", hit_row, product, precision=lax.Precision.HIGHEST)
    return placed.reshape(RB * TB, panel_count * RB * TB)


def per_device(tiles, tile_rows, tile_cols, counts, scaling):
    slot_total = tiles.shape[1]
    slot_range = jnp.arange(slot_total, dtype=jnp.int32)
    own_live = (slot_range < counts[0, 0]).astype(jnp.float32)
    blocked = densify(
        tiles[0], tile_rows[0], tile_cols[0], own_live, scaling.reshape(CB_DEV, TB), CB_DEV
    )
    piece_tiles = lax.all_gather(tiles, "rows", axis=0, tiled=True)
    piece_rows = lax.all_gather(tile_rows, "rows", axis=0, tiled=True)
    piece_cols = lax.all_gather(tile_cols, "rows", axis=0, tiled=True)
    piece_counts = lax.all_gather(counts, "rows", axis=0, tiled=True)
    count_here = piece_tiles.shape[0]
    live_mask = (slot_range[None, :] < piece_counts).astype(jnp.float32).reshape(-1)
    tile_block = place_panels(
        blocked,
        piece_tiles.reshape(count_here * slot_total, TB, TB),
        piece_rows.reshape(-1),
        piece_cols.reshape(-1),
        live_mask,
        count_here,
    )
    return lax.psum_scatter(tile_block, "cols", scatter_dimension=1, tiled=True)


def solution(mesh):
    placed = (
        P("rows", "cols", None, None),
        P("rows", "cols"),
        P("rows", "cols"),
        P("rows", "cols"),
        P("cols"),
    )
    return jax.shard_map(
        per_device, mesh=mesh, in_specs=placed, out_specs=P("rows", "cols"), check_vma=False
    )
```

profile of v0, /device:TPU:1, one launch (start us, length us, event | category | flops | bytes accessed | tf_op | source)
XLA Modules:
  0.0 301.7 jit_solution(16570171646516832178)
XLA Ops:
  6.5 0.0 all-gather.4.cloned.1.call-start
  6.5 0.7 all-gather.4.cloned.1.call-update
  7.3 0.0 reduce-scatter.2.cloned.1.call-start
  8.0 23.1 %all-gather = s32[32,1,8]{2,1,0:T(1,128)S(1)} all-gather(s32[1,1,8]{2,1,0:T(1,128)} %bitcast.44), channel_id=1, replica_groups=mesh['rows'=32,'cols'=8] {'rows'}, dimensions={0}, use_global_device_ids=true | all-gather | bytes 1056 | tf_op jit(solution)/shard_map/all_gather | solution.py:39
  31.1 0.1 reshape.142
  31.1 0.6 broadcast.123
  31.7 0.7 reduce.5
  32.5 0.1 reshape.140
  32.6 0.7 fusion.17
  33.3 1.2 bitcast_multiply_fusion
  34.4 0.2 broadcast_in_dim.19
  34.7 1.1 scatter_fusion
  35.8 0.0 copy-start
  35.8 1.3 copy-done
  37.1 1.8 broadcast_multiply_fusion
  38.9 0.0 copy-start.2
  38.9 0.0 copy-start.1
  38.9 12.4 %gather_fusion = f32[256,256,128]{2,1,0:T(8,128)} fusion(f32[16,256,128]{2,1,0:T(8,128)S(1)} %bitcast.36, s32[1024]{0:T(1024)S(1)} %pad_clamp_fusion), kind=kCustom, calls=%fused_computation | custom fusion | bytes 67109888 | tf_op jit(solution)/shard_map/jit(_take)/gather | solution.py:19
  51.3 0.0 copy-done.2
  51.3 0.6 dynamic-slice
  52.0 0.7 bitcast_dynamic-update-slice_fusion
  52.7 12.0 %all-reduce = s32[32]{0:T(128)S(1)} all-reduce(s32[32]{0:T(128)S(1)} %bitcast_dynamic-update-slice_fusion), channel_id=1, replica_groups=mesh['rows'=32,'cols'=8] {'rows'}, use_global_device_ids=true, to_apply=%add | all-reduce | flops 32 | bytes 256
  64.7 0.0 copy-done.1
  64.7 22.6 %all-gather.1 = s32[32,1,8]{2,1,0:T(1,128)S(1)} all-gather(s32[1,1,8]{2,1,0:T(1,128)S(1)} %bitcast.45), channel_id=1, replica_groups=mesh['rows'=32,'cols'=8] {'rows'}, dimensions={0}, use_global_device_ids=true | all-gather | bytes 1056 | tf_op jit(solution)/shard_map/all_gather | solution.py:38
  87.3 0.1 fusion.15
  87.4 4.4 %all-gather.4.cloned.1.call-done = f32[32,8,128,128]{3,2,1,0:T(8,128)} async-done(((f32[1,8,128,128]{3,2,1,0:T(8,128)}), f32[32,8,128,128]{3,2,1,0:T(8,128)}) %all-gather.4.cloned.1.call-update) | async-done | bytes 16777232 | tf_op jit(solution)/shard_map/all_gather | solution.py:37
  91.8 38.0 %fusion.2 = f32[256,256,128]{2,1,0:T(8,128)} fusion(f32[256,128,128]{2,1,0:T(8,128)} %bitcast.39, f32[256,256,128]{2,1,0:T(8,128)} %gather_fusion, pred[256]{0:T(512)(128)(4,1)S(1)} %compare_and_fusion), kind=kOutput, calls=%fused_computation.4 | convolution fusion | flops 12893290496 | bytes 83886336 | tf_op jit(solution)/shard_map/kac,kbc->kab/dot_general | solution.py:20
  129.8 55.1 %fusion.6 = f32[256,32,2,128]{3,2,0,1:T(2,128)} fusion(f32[32,8,256,128]{3,2,1,0:T(8,128)} %bitcast.37, f32[32,8]{1,0:T(8,128)S(1)} %fusion.15, s32[32,8]{1,0:T(8,128)S(1)} %bitcast.40), kind=kOutput, calls=%fused_computation.8 | convolution fusion | flops 201327616 | bytes 41945088 | tf_op jit(solution)/shard_map/pkr,pkab->aprb/dot_general | solution.py:26
  184.9 13.1 %copy.11 = f32[256,32,2,128]{0,3,2,1:T(8,128)} copy(f32[256,32,2,128]{3,2,0,1:T(2,128)} %fusion.6) | data formatting | bytes 16777216 | tf_op jit(solution)/shard_map/pkr,pkab->aprb/transpose | solution.py:26
  198.0 0.0 reduce-scatter.2.cloned.1.call-update
  198.0 94.3 %reduce-scatter.2.cloned.1.call-done = f32[256,1024]{0,1:T(8,128)} async-done(((f32[256,8192]{0,1:T(8,128)}), f32[256,1024]{0,1:T(8,128)}) %reduce-scatter.2.cloned.1.call-update) | async-done | bytes 1048592 | tf_op jit(solution)/shard_map/reduce_scatter | solution.py:51
  292.3 2.5 copy.12
  (5 shorter events, 0.0 us)
Async XLA Ops:
  6.5 85.3 %all-gather.4.cloned.1.call-start = ((), (), s32[]{:S(2)}) async-start(), calls=%async_computation.1 | async-start | bytes 17301504 | tf_op jit(solution)/shard_map/all_gather | solution.py:37
  7.3 285.1 %reduce-scatter.2.cloned.1.call-start = ((), (), s32[]{:S(2)}) async-start(), calls=%async_computation.2 | async-start | bytes 9437184 | tf_op jit(solution)/shard_map/reduce_scatter | solution.py:51
  35.8 1.4 copy-start
  38.9 12.4 %copy-start.2 = (u32[256]{0:T(256)S(1)}, u32[256]{0:T(256)}, u32[]{:S(2)}) copy-start(u32[256]{0:T(256)} %constant.45) | copy-start | bytes 3076
  38.9 25.8 %copy-start.1 = (s32[1,8]{1,0:T(1,128)S(1)}, s32[1,8]{1,0:T(1,128)}, u32[]{:S(2)}) copy-start(s32[1,8]{1,0:T(1,128)} %param.6) | copy-start | bytes 100
Sparse Core Ops, SparseCore 0:
  9.9 81.8 all-gather.3
  198.2 94.1 reduce-scatter.1
where the time goes:
time: 302 us
  waiting for transfers between devices  99.5 us (33%)
  matrix products  93.1 us (31%)
  blocking collectives  57.7 us (19%)
  local copies, waits for them, and re-layouts  31.7 us (10%)
  between operations  14.2 us (5%)
  other arithmetic  5.55 us (2%)
    reduce_scatter x1, waiting for transfers between devices, per_device(): return lax.psum_scatter(tile_block, 'cols', scatter_dimension=1, tiled=True)  94.3 us
    dot_general x1, matrix products, place_panels(): jnp.einsum('pkr,pkab->aprb', hit_row, product, precision=lax.Precision.HI...  55.1 us
    dot_general x1, matrix products, place_panels(): jnp.einsum('kac,kbc->kab', picked, tile_set, precision=lax.Precision.HIGH...  38 us
    all_gather x1, blocking collectives, per_device(): piece_cols = lax.all_gather(tile_cols, 'rows', axis=0, tiled=True)  23.1 us
    all_gather x1, blocking collectives, per_device(): piece_rows = lax.all_gather(tile_rows, 'rows', axis=0, tiled=True)  22.6 us
    transpose x1, local copies, waits for them, and re-layouts, place_panels(): jnp.einsum('pkr,pkab->aprb', hit_row, product, precision=lax.Precision.HI...  13.1 us
    gather x1, local copies, waits for them, and re-layouts, place_panels(): picked = jnp.take(blocked, col_ids, axis=0)  12.4 us
    unnamed x1, blocking collectives  12 us
  transfers between devices with their start and end apart: 2, of which 2 were waited for; matrix products, arithmetic and copies ran while one was open for 7% of the time, Pallas kernels for 0%

commit v1 on v0

v1 whole, which is shorter than its diff:
```python
import functools

import jax
import jax.numpy as jnp
from jax import lax
from jax.experimental import pallas as pl
from jax.experimental.pallas import tpu as pltpu
from jax.sharding import PartitionSpec as P

TB = 128
RB = 2
CB_DEV = 16
META = 8


def pack(tiles, tile_rows, tile_cols, counts):
    slots = tiles.shape[1]
    meta = jnp.stack(
        [tile_rows[0], tile_cols[0], jnp.broadcast_to(counts[0, 0], (slots,))]
    ).astype(jnp.float32)
    meta = jnp.pad(meta, ((0, META - 3), (0, TB - slots)))
    return jnp.concatenate([tiles[0].reshape(slots * TB, TB), meta], axis=0)


def unpack_meta(sets, slots):
    return sets[:, slots * TB : slots * TB + 3, :slots].astype(jnp.int32).reshape(-1)


def split(x):
    hi = x.astype(jnp.bfloat16)
    lo = (x - hi.astype(jnp.float32)).astype(jnp.bfloat16)
    return hi, lo


def dot_t(a, b):
    return lax.dot_general(a, b, (((1,), (1,)), ((), ())), preferred_element_type=jnp.float32)


def normal_kernel(slots, far_per, own_meta, far_meta, own_ref, far_ref, scal_ref, out_ref, dense, p_hi, p_lo):
    g = pl.program_id(0)

    @pl.when(g == 0)
    def _():
        out_ref[...] = jnp.zeros_like(out_ref)

    dense[...] = jnp.zeros_like(dense)
    own_count = own_meta[(g * 3 + 2) * slots]
    for k in range(slots):

        @pl.when(k < own_count)
        def _():
            r = own_meta[(g * 3 + 0) * slots + k]
            c = own_meta[(g * 3 + 1) * slots + k]
            rows = pl.ds(pl.multiple_of(r * TB, TB), TB)
            cols = pl.ds(pl.multiple_of(c * TB, TB), TB)
            tile = own_ref[0, k * TB : (k + 1) * TB, :]
            dense[rows, cols] += tile * scal_ref[0, pl.ds(c, 1), :]

    hi, lo = split(dense[...])
    p_hi[...] = hi
    p_lo[...] = lo

    def body(t, carry):
        qi = t // slots
        k = t % slots
        base = (g * far_per + qi) * 3 * slots
        count = far_meta[base + 2 * slots]

        @pl.when(k < count)
        def _():
            r = far_meta[base + k]
            c = far_meta[base + slots + k]
            cols = pl.ds(pl.multiple_of(c * TB, TB), TB)
            tile = far_ref[qi, pl.ds(pl.multiple_of(k * TB, TB), TB), :]
            t_hi, t_lo = split(tile)
            a_hi = p_hi[:, cols]
            a_lo = p_lo[:, cols]
            prod = dot_t(a_hi, t_hi) + (dot_t(a_hi, t_lo) + dot_t(a_lo, t_hi))
            dest = pl.ds(pl.multiple_of(qi * RB * TB + r * TB, TB), TB)
            out_ref[:, dest] += prod

        return carry

    lax.fori_loop(0, far_per * slots, body, 0)


def per_device(tiles, tile_rows, tile_cols, counts, scaling):
    n_rows = lax.axis_size("rows")
    n_cols = lax.axis_size("cols")
    slots = tiles.shape[1]
    far_per = n_rows // n_cols
    packed = pack(tiles, tile_rows, tile_cols, counts)
    set_len = packed.shape[0]

    perm = []
    for q in range(n_rows):
        for gp in range(n_cols):
            dst_r = gp * far_per + q % far_per
            dst_c = q // far_per
            perm.append((q * n_cols + gp, dst_r * n_cols + dst_c))
    moved = lax.ppermute(packed, ("rows", "cols"), perm)
    far = lax.all_gather(moved[None], "rows", axis=0, tiled=True)
    own = lax.all_gather(packed[None], "cols", axis=0, tiled=True)
    scal = lax.all_gather(scaling, "cols", axis=0, tiled=True).reshape(n_cols, CB_DEV, TB)

    own_meta = unpack_meta(own, slots)
    far_meta = unpack_meta(far, slots)
    out_cols = far_per * RB * TB

    grid_spec = pltpu.PrefetchScalarGridSpec(
        num_scalar_prefetch=2,
        grid=(n_cols,),
        in_specs=[
            pl.BlockSpec((1, set_len, TB), lambda g, om, fm: (g, 0, 0)),
            pl.BlockSpec((far_per, set_len, TB), lambda g, om, fm: (g, 0, 0)),
            pl.BlockSpec((1, CB_DEV, TB), lambda g, om, fm: (g, 0, 0)),
        ],
        out_specs=pl.BlockSpec((RB * TB, out_cols), lambda g, om, fm: (0, 0)),
        scratch_shapes=[
            pltpu.VMEM((RB * TB, CB_DEV * TB), jnp.float32),
            pltpu.VMEM((RB * TB, CB_DEV * TB), jnp.bfloat16),
            pltpu.VMEM((RB * TB, CB_DEV * TB), jnp.bfloat16),
        ],
    )
    return pl.pallas_call(
        functools.partial(normal_kernel, slots, far_per),
        grid_spec=grid_spec,
        out_shape=jax.ShapeDtypeStruct((RB * TB, out_cols), jnp.float32),
        compiler_params=pltpu.CompilerParams(dimension_semantics=("arbitrary",)),
    )(own_meta, far_meta, own, far, scal)


def solution(mesh):
    placed = (
        P("rows", "cols", None, None),
        P("rows", "cols"),
        P("rows", "cols"),
        P("rows", "cols"),
        P("cols"),
    )
    return jax.shard_map(
        per_device, mesh=mesh, in_specs=placed, out_specs=P("rows", "cols"), check_vma=False
    )
```

time: 302 us -> 243 us (0.80)
  the two profiles are of different devices: /device:TPU:1 before, /device:TPU:161 now
where the time goes in v1:
time: 243 us
  waiting for transfers between devices  125 us (51%)
  Pallas kernels  51 us (21%)
  blocking collectives  41.3 us (17%)
  between operations  14.1 us (6%)
  starting transfers between devices  5.05 us (2%)
  other arithmetic  4.29 us (2%)
    all_gather x1, waiting for transfers between devices, per_device(): far = lax.all_gather(moved[None], 'rows', axis=0, tiled=True)  86.5 us
    pallas_call x1, Pallas kernels, per_device(): pl.pallas_call(functools.partial(normal_kernel, slots, far_per), grid_spe...  51 us
    all_gather x1, blocking collectives, per_device(): lax.all_gather(scaling, 'cols', axis=0, tiled=True)  41.3 us
    ppermute x1, waiting for transfers between devices, per_device(): moved = lax.ppermute(packed, ('rows', 'cols'), perm)  38.5 us
    ppermute x1, starting transfers between devices, per_device(): moved = lax.ppermute(packed, ('rows', 'cols'), perm)  5.01 us
  transfers between devices with their start and end apart: 3, of which 2 were waited for; matrix products, arithmetic and copies ran while one was open for 1% of the time, Pallas kernels for 0%

profile of v1, /device:TPU:161, one launch (start us, length us, event | category | flops | bytes accessed | tf_op | source)
XLA Modules:
  0.0 243.0 jit_solution(15030231403076282352)
XLA Ops:
  6.5 0.0 all-gather.5.cloned.1.call-start
  7.2 0.1 pad.9.clone
  7.3 0.7 add_convert_fusion
  8.0 1.9 select_maximum_fusion
  9.9 0.0 all-gather.5.cloned.1.call-update
  9.9 0.0 all-gather.7.cloned.1.call-start
  9.9 5.0 %collective-permute-start = (f32[1032,128]{1,0:T(8,128)}, f32[1032,128]{1,0:T(8,128)S(1)}, u32[]{:S(2)}, u32[]{:S(2)}) collective-permute-start(f32[1032,128]{1,0:T(8,128)} %select_maximum_fusion), channel_id=1, source_target_pairs={{0,0},{1,32},{2,64},{3,96},{4,128},{5,160},{6,192},{7,224},{8,8},{... | collective-permute-start | bytes 1585160 | tf_op jit(solution)/shard_map/ppermute | solution.py:101
  15.0 38.5 %collective-permute-done = f32[1032,128]{1,0:T(8,128)S(1)} collective-permute-done((f32[1032,128]{1,0:T(8,128)}, f32[1032,128]{1,0:T(8,128)S(1)}, u32[]{:S(2)}, u32[]{:S(2)}) %collective-permute-start) | collective-permute-done | bytes 528416 | tf_op jit(solution)/shard_map/ppermute | solution.py:101
  53.4 0.0 copy-start
  53.4 0.8 copy-done
  54.2 0.0 all-gather.7.cloned.1.call-update
  54.2 41.3 %all_gather.11 = f32[16384]{0:T(1024)} all-gather(f32[2048]{0:T(1024)} %param.9), channel_id=1, replica_groups=mesh['rows'=32,'cols'=8] {'cols'}, dimensions={0}, use_global_device_ids=true | all-gather | bytes 73728 | tf_op jit(solution)/shard_map/all_gather | solution.py:104
  95.6 0.0 all-gather.5.cloned.1.call-done
  95.6 0.8 slice_convert_fusion.1
  96.3 0.7 reshape.9.own_meta
  97.0 86.5 %all-gather.7.cloned.1.call-done = f32[33024,128]{1,0:T(8,128)} async-done(((f32[1032,128]{1,0:T(8,128)}), f32[33024,128]{1,0:T(8,128)}) %all-gather.7.cloned.1.call-update) | async-done | bytes 16908304 | tf_op jit(solution)/shard_map/all_gather | solution.py:102
  183.5 0.9 slice_convert_fusion
  184.4 0.7 reshape.10.far_meta
  185.1 51.0 %shard_map.55 = f32[256,1024]{1,0:T(8,128)} custom-call(s32[192]{0:T(256)} %reshape.9.own_meta, s32[768]{0:T(1024)} %reshape.10.far_meta, f32[8,1032,128]{2,1,0:T(8,128)} %bitcast.11, f32[32,1032,128]{2,1,0:T(8,128)} %bitcast.9, f32[8,16,128]{2,1,0:T(8,128)} %bitcast.13), custom_call_target="tpu_custom_call" | custom-call | tf_op jit(solution)/shard_map/pallas_call | solution.py:125
Async XLA Ops:
  6.5 89.0 %all-gather.5.cloned.1.call-start = ((), (), s32[]{:S(2)}) async-start(), calls=%async_computation | async-start | bytes 4755456 | tf_op jit(solution)/shard_map/all_gather | solution.py:103
  9.9 173.6 %all-gather.7.cloned.1.call-start = ((), (), s32[]{:S(2)}) async-start(), calls=%async_computation.1 | async-start | bytes 17436672 | tf_op jit(solution)/shard_map/all_gather | solution.py:102
  9.9 43.5 %collective-permute-start = (f32[1032,128]{1,0:T(8,128)}, f32[1032,128]{1,0:T(8,128)S(1)}, u32[]{:S(2)}, u32[]{:S(2)}) collective-permute-start(f32[1032,128]{1,0:T(8,128)} %select_maximum_fusion), channel_id=1, source_target_pairs={{0,0},{1,32},{2,64},{3,96},{4,128},{5,160},{6,192},{7,224},{8,8},{... | collective-permute-start | bytes 1585160 | tf_op jit(solution)/shard_map/ppermute | solution.py:101
  53.4 0.8 copy-start
Sparse Core Ops, SparseCore 0:
  10.0 84.9 all-gather.4
  97.7 85.7 all-gather.6

commit v2 on v1

--- a/solution.py
+++ b/solution.py
@@ -11,19 +11,84 @@
 RB = 2
 CB_DEV = 16
 META = 8
-
-
-def pack(tiles, tile_rows, tile_cols, counts):
+MESH = pl.DeviceIdType.MESH
+
+
+def pack(tiles, tile_rows, tile_cols, counts, scaling=None):
     slots = tiles.shape[1]
     meta = jnp.stack(
         [tile_rows[0], tile_cols[0], jnp.broadcast_to(counts[0, 0], (slots,))]
     ).astype(jnp.float32)
     meta = jnp.pad(meta, ((0, META - 3), (0, TB - slots)))
-    return jnp.concatenate([tiles[0].reshape(slots * TB, TB), meta], axis=0)
+    parts = [tiles[0].reshape(slots * TB, TB), meta]
+    if scaling is not None:
+        parts += [scaling.reshape(CB_DEV, TB), jnp.zeros((META, TB), jnp.float32)]
+    return jnp.concatenate(parts, axis=0)
 
 
 def unpack_meta(sets, slots):
     return sets[:, slots * TB : slots * TB + 3, :slots].astype(jnp.int32).reshape(-1)
+
+
+def ring_kernel(n, half, x_ref, out_ref, local_sem, send_sem, recv_sem):
+    me = lax.axis_index("cols")
+    row = lax.axis_index("rows")
+    right = lax.rem(me + 1, n)
+    left = lax.rem(me + n - 1, n)
+    barrier = pltpu.get_barrier_semaphore()
+    for neighbour in (left, right):
+        pl.semaphore_signal(barrier, inc=1, device_id=(row, neighbour), device_id_type=MESH)
+    pl.semaphore_wait(barrier, 2)
+
+    local = pltpu.make_async_copy(x_ref, out_ref.at[me], local_sem)
+    local.start()
+    halves = (pl.ds(0, half), pl.ds(half, half))
+    targets = (right, left)
+    previous = [None, None]
+    for step in range(n - 1):
+        for way in range(2):
+            if way == 0:
+                origin = lax.rem(me - step + n, n)
+            else:
+                origin = lax.rem(me + step, n)
+            if step == 0:
+                src_ref = x_ref.at[halves[way]]
+            else:
+                previous[way].wait_recv()
+                src_ref = out_ref.at[origin, halves[way]]
+            copy = pltpu.make_async_remote_copy(
+                src_ref=src_ref,
+                dst_ref=out_ref.at[origin, halves[way]],
+                send_sem=send_sem.at[way, step],
+                recv_sem=recv_sem.at[way, step],
+                device_id=(row, targets[way]),
+                device_id_type=MESH,
+            )
+            copy.start()
+            if previous[way] is not None:
+                previous[way].wait_send()
+            previous[way] = copy
+    for way in range(2):
+        previous[way].wait_recv()
+        previous[way].wait_send()
+    local.wait()
+
+
+def ring_gather(x, n):
+    rows = x.shape[0]
+    return pl.pallas_call(
+        functools.partial(ring_kernel, n, rows // 2),
+        out_shape=jax.ShapeDtypeStruct((n,) + x.shape, x.dtype),
+        in_specs=[pl.BlockSpec(memory_space=pl.ANY)],
+        out_specs=pl.BlockSpec(memory_space=pl.ANY),
+        scratch_shapes=[
+            pltpu.SemaphoreType.DMA(()),
+            pltpu.SemaphoreType.DMA((2, n - 1)),
+            pltpu.SemaphoreType.DMA((2, n - 1)),
+        ],
+        compiler_params=pltpu.CompilerParams(collective_id=0, has_side_effects=True),
+        cost_estimate=pl.CostEstimate(flops=0, bytes_accessed=2 * n * x.size * 4, transcendentals=0),
+    )(x)
 
 
 def split(x):
@@ -36,7 +101,7 @@
     return lax.dot_general(a, b, (((1,), (1,)), ((), ())), preferred_element_type=jnp.float32)
 
 
-def normal_kernel(slots, far_per, own_meta, far_meta, own_ref, far_ref, scal_ref, out_ref, dense, p_hi, p_lo):
+def normal_kernel(slots, far_per, own_meta, far_meta, own_ref, far_ref, out_ref, dense, p_hi, p_lo):
     g = pl.program_id(0)
 
     @pl.when(g == 0)
@@ -54,7 +119,7 @@
             rows = pl.ds(pl.multiple_of(r * TB, TB), TB)
             cols = pl.ds(pl.multiple_of(c * TB, TB), TB)
             tile = own_ref[0, k * TB : (k + 1) * TB, :]
-            dense[rows, cols] += tile * scal_ref[0, pl.ds(c, 1), :]
+            dense[rows, cols] += tile * own_ref[0, pl.ds(slots * TB + META + c, 1), :]
 
     hi, lo = split(dense[...])
     p_hi[...] = hi
@@ -91,6 +156,8 @@
     far_per = n_rows // n_cols
     packed = pack(tiles, tile_rows, tile_cols, counts)
     set_len = packed.shape[0]
+    own_packed = pack(tiles, tile_rows, tile_cols, counts, scaling)
+    own_len = own_packed.shape[0]
 
     perm = []
     for q in range(n_rows):
@@ -100,8 +167,7 @@
             perm.append((q * n_cols + gp, dst_r * n_cols + dst_c))
     moved = lax.ppermute(packed, ("rows", "cols"), perm)
     far = lax.all_gather(moved[None], "rows", axis=0, tiled=True)
-    own = lax.all_gather(packed[None], "cols", axis=0, tiled=True)
-    scal = lax.all_gather(scaling, "cols", axis=0, tiled=True).reshape(n_cols, CB_DEV, TB)
+    own = ring_gather(own_packed, n_cols)
 
     own_meta = unpack_meta(own, slots)
     far_meta = unpack_meta(far, slots)
@@ -111,9 +177,8 @@
         num_scalar_prefetch=2,
         grid=(n_cols,),
         in_specs=[
-            pl.BlockSpec((1, set_len, TB), lambda g, om, fm: (g, 0, 0)),
+            pl.BlockSpec((1, own_len, TB), lambda g, om, fm: (g, 0, 0)),
             pl.BlockSpec((far_per, set_len, TB), lambda g, om, fm: (g, 0, 0)),
-            pl.BlockSpec((1, CB_DEV, TB), lambda g, om, fm: (g, 0, 0)),
         ],
         out_specs=pl.BlockSpec((RB * TB, out_cols), lambda g, om, fm: (0, 0)),
         scratch_shapes=[
@@ -127,7 +192,7 @@
         grid_spec=grid_spec,
         out_shape=jax.ShapeDtypeStruct((RB * TB, out_cols), jnp.float32),
         compiler_params=pltpu.CompilerParams(dimension_semantics=("arbitrary",)),
-    )(own_meta, far_meta, own, far, scal)
+    )(own_meta, far_meta, own, far)
 
 
 def solution(mesh):

time: 243 us -> 206 us (0.85)
  the two profiles are of different devices: /device:TPU:161 before, /device:TPU:103 now
where the time goes in v2:
time: 206 us
  Pallas kernels  117 us (57%)
  waiting for transfers between devices  64.8 us (31%)
  between operations  14.1 us (7%)
  other arithmetic  5.56 us (3%)
  local copies, waits for them, and re-layouts  2.31 us (1%)
  starting transfers between devices  2.3 us (1%)
    pallas_call x1, Pallas kernels, ring_gather(): pl.pallas_call(functools.partial(ring_kernel, n, rows // 2), out_shape=ja...  66.2 us
    pallas_call x1, Pallas kernels, per_device(): pl.pallas_call(functools.partial(normal_kernel, slots, far_per), grid_spe...  50.8 us
    ppermute x1, waiting for transfers between devices, per_device(): moved = lax.ppermute(packed, ('rows', 'cols'), perm)  34 us
    all_gather x1, waiting for transfers between devices, per_device(): far = lax.all_gather(moved[None], 'rows', axis=0, tiled=True)  30.8 us
  transfers between devices with their start and end apart: 2, of which 2 were waited for; matrix products, arithmetic and copies ran while one was open for 2% of the time, Pallas kernels for 32%

profile of v2, /device:TPU:103, one launch (start us, length us, event | category | flops | bytes accessed | tf_op | source)
XLA Modules:
  0.0 206.1 jit_solution(11350277790956542858)
XLA Ops:
  6.5 0.0 all-gather.3.cloned.1.call-start
  7.2 0.1 pad.14.clone
  7.3 0.7 add_convert_fusion
  8.0 1.1 pad_maximum_fusion
  9.1 2.3 %collective-permute-start = (f32[1032,128]{1,0:T(8,128)S(1)}, f32[1032,128]{1,0:T(8,128)S(1)}, u32[]{:S(2)}, u32[]{:S(2)}) collective-permute-start(f32[1032,128]{1,0:T(8,128)S(1)} %pad_maximum_fusion), channel_id=1, source_target_pairs={{0,0},{1,32},{2,64},{3,96},{4,128},{5,160},{6,192},{7,224},{8,8},{... | collective-permute-start | bytes 1585160 | tf_op jit(solution)/shard_map/ppermute | solution.py:168
  11.4 34.0 %collective-permute-done = f32[1032,128]{1,0:T(8,128)S(1)} collective-permute-done((f32[1032,128]{1,0:T(8,128)S(1)}, f32[1032,128]{1,0:T(8,128)S(1)}, u32[]{:S(2)}, u32[]{:S(2)}) %collective-permute-start) | collective-permute-done | bytes 528416 | tf_op jit(solution)/shard_map/ppermute | solution.py:168
  45.4 0.0 copy-start
  45.4 0.8 copy-done
  46.2 0.0 all-gather.3.cloned.1.call-update
  46.2 0.1 pad.11.clone
  46.3 2.1 %maximum_maximum_fusion.x_ref = f32[1056,128]{1,0:T(8,128)} fusion(f32[16,128]{1,0:T(8,128)} %bitcast.11, f32[8,128]{1,0:T(8,128)S(1)} %pad.5, f32[1024,128]{1,0:T(8,128)} %bitcast.10, f32[1056]{0:T(1024)S(1)} %pad.11.clone), kind=kLoop, calls=%fused_computation | loop fusion | flops 405504 | bytes 1081472 | tf_op jit(solution)/shard_map/concatenate | solution.py:26
  48.4 66.2 %shard_map.55.own_ref = f32[8,1056,128]{2,1,0:T(8,128)} custom-call(f32[1056,128]{1,0:T(8,128)} %maximum_maximum_fusion.x_ref), custom_call_target="tpu_custom_call" | custom-call | bytes 8650752 | tf_op jit(solution)/shard_map/pallas_call | solution.py:79
  114.6 0.8 slice_convert_fusion.1
  115.3 0.7 reshape.10.own_meta
  116.0 30.8 %all-gather.3.cloned.1.call-done = f32[33024,128]{1,0:T(8,128)} async-done(((f32[1032,128]{1,0:T(8,128)}), f32[33024,128]{1,0:T(8,128)}) %all-gather.3.cloned.1.call-update) | async-done | bytes 16908304 | tf_op jit(solution)/shard_map/all_gather | solution.py:169
  146.8 0.9 slice_convert_fusion
  147.8 0.7 reshape.11.far_meta
  148.4 50.8 %shard_map.56 = f32[256,1024]{1,0:T(8,128)} custom-call(s32[192]{0:T(256)} %reshape.10.own_meta, s32[768]{0:T(1024)} %reshape.11.far_meta, f32[8,1056,128]{2,1,0:T(8,128)} %shard_map.55.own_ref, f32[32,1032,128]{2,1,0:T(8,128)} %bitcast.8), custom_call_target="tpu_custom_call" | custom-call | tf_op jit(solution)/shard_map/pallas_call | solution.py:190
  (2 shorter events, 0.0 us)
Async XLA Ops:
  6.5 140.3 %all-gather.3.cloned.1.call-start = ((), (), s32[]{:S(2)}) async-start(), calls=%async_computation | async-start | bytes 17436672 | tf_op jit(solution)/shard_map/all_gather | solution.py:169
  9.1 36.3 %collective-permute-start = (f32[1032,128]{1,0:T(8,128)S(1)}, f32[1032,128]{1,0:T(8,128)S(1)}, u32[]{:S(2)}, u32[]{:S(2)}) collective-permute-start(f32[1032,128]{1,0:T(8,128)S(1)} %pad_maximum_fusion), channel_id=1, source_target_pairs={{0,0},{1,32},{2,64},{3,96},{4,128},{5,160},{6,192},{7,224},{8,8},{... | collective-permute-start | bytes 1585160 | tf_op jit(solution)/shard_map/ppermute | solution.py:168
  45.4 0.8 copy-start
Sparse Core Ops, SparseCore 0:
  46.3 100.4 all-gather.2

commit v3 on v2

--- a/solution.py
+++ b/solution.py
@@ -101,7 +101,7 @@
     return lax.dot_general(a, b, (((1,), (1,)), ((), ())), preferred_element_type=jnp.float32)
 
 
-def normal_kernel(slots, far_per, own_meta, far_meta, own_ref, far_ref, out_ref, dense, p_hi, p_lo):
+def normal_kernel(slots, far_per, own_meta, far_meta, own_ref, far_ref, out_ref, dense, p_hi, p_lo, x_hi, x_lo, z_hi, z_lo):
     g = pl.program_id(0)
 
     @pl.when(g == 0)
@@ -125,28 +125,25 @@
     p_hi[...] = hi
     p_lo[...] = lo
 
-    def body(t, carry):
-        qi = t // slots
-        k = t % slots
+    for qi in range(far_per):
         base = (g * far_per + qi) * 3 * slots
         count = far_meta[base + 2 * slots]
-
-        @pl.when(k < count)
-        def _():
+        for k in range(slots):
             r = far_meta[base + k]
-            c = far_meta[base + slots + k]
-            cols = pl.ds(pl.multiple_of(c * TB, TB), TB)
-            tile = far_ref[qi, pl.ds(pl.multiple_of(k * TB, TB), TB), :]
-            t_hi, t_lo = split(tile)
-            a_hi = p_hi[:, cols]
-            a_lo = p_lo[:, cols]
-            prod = dot_t(a_hi, t_hi) + (dot_t(a_hi, t_lo) + dot_t(a_lo, t_hi))
-            dest = pl.ds(pl.multiple_of(qi * RB * TB + r * TB, TB), TB)
-            out_ref[:, dest] += prod
-
-        return carry
-
-    lax.fori_loop(0, far_per * slots, body, 0)
+            c = jnp.minimum(jnp.maximum(far_meta[base + slots + k], 0), CB_DEV - 1)
+            src = pl.ds(pl.multiple_of(c * TB, TB), TB)
+            x_hi[:, k * TB : (k + 1) * TB] = p_hi[:, src]
+            x_lo[:, k * TB : (k + 1) * TB] = p_lo[:, src]
+            t_hi, t_lo = split(far_ref[qi, k * TB : (k + 1) * TB, :])
+            live = k < count
+            for half in range(RB):
+                keep = jnp.logical_and(live, r == half)
+                z_hi[half * TB : (half + 1) * TB, k * TB : (k + 1) * TB] = jnp.where(keep, t_hi, jnp.zeros_like(t_hi))
+                z_lo[half * TB : (half + 1) * TB, k * TB : (k + 1) * TB] = jnp.where(keep, t_lo, jnp.zeros_like(t_lo))
+        a_hi = x_hi[...]
+        b_hi = z_hi[...]
+        prod = dot_t(a_hi, b_hi) + (dot_t(a_hi, z_lo[...]) + dot_t(x_lo[...], b_hi))
+        out_ref[:, qi * RB * TB : (qi + 1) * RB * TB] += prod
 
 
 def per_device(tiles, tile_rows, tile_cols, counts, scaling):
@@ -185,6 +182,10 @@
             pltpu.VMEM((RB * TB, CB_DEV * TB), jnp.float32),
             pltpu.VMEM((RB * TB, CB_DEV * TB), jnp.bfloat16),
             pltpu.VMEM((RB * TB, CB_DEV * TB), jnp.bfloat16),
+            pltpu.VMEM((RB * TB, slots * TB), jnp.bfloat16),
+            pltpu.VMEM((RB * TB, slots * TB), jnp.bfloat16),
+            pltpu.VMEM((RB * TB, slots * TB), jnp.bfloat16),
+            pltpu.VMEM((RB * TB, slots * TB), jnp.bfloat16),
         ],
     )
     return pl.pallas_call(

time: 206 us -> 192 us (0.932)
  the two profiles are of different devices: /device:TPU:103 before, /device:TPU:1 now
where the time goes in v3:
time: 192 us
  Pallas kernels  144 us (75%)
  waiting for transfers between devices  25.7 us (13%)
  between operations  14.1 us (7%)
  other arithmetic  5.56 us (3%)
  local copies, waits for them, and re-layouts  2.3 us (1%)
    pallas_call x1, Pallas kernels, ring_gather(): pl.pallas_call(functools.partial(ring_kernel, n, rows // 2), out_shape=ja...  109 us
    pallas_call x1, Pallas kernels, per_device(): pl.pallas_call(functools.partial(normal_kernel, slots, far_per), grid_spe...  34.6 us
    all_gather x1, waiting for transfers between devices, per_device(): far = lax.all_gather(moved[None], 'rows', axis=0, tiled=True)  25.7 us
  transfers between devices with their start and end apart: 2, of which 1 were waited for; matrix products, arithmetic and copies ran while one was open for 2% of the time, Pallas kernels for 57%

profile of v3, /device:TPU:1, one launch (start us, length us, event | category | flops | bytes accessed | tf_op | source)
XLA Modules:
  0.0 191.9 jit_solution(6368902979162362362)
XLA Ops:
  6.5 0.0 all-gather.3.cloned.1.call-start
  7.2 0.1 pad.14.clone
  7.3 0.7 add_convert_fusion
  8.0 1.1 pad_maximum_fusion
  9.1 0.7 collective-permute-start
  9.8 0.0 collective-permute-done
  9.8 0.0 copy-start
  9.8 0.8 copy-done
  10.6 0.0 all-gather.3.cloned.1.call-update
  10.6 0.1 pad.11.clone
  10.7 2.1 %maximum_maximum_fusion.x_ref = f32[1056,128]{1,0:T(8,128)} fusion(f32[16,128]{1,0:T(8,128)} %bitcast.11, f32[8,128]{1,0:T(8,128)S(1)} %pad.5, f32[1024,128]{1,0:T(8,128)} %bitcast.10, f32[1056]{0:T(1024)S(1)} %pad.11.clone), kind=kLoop, calls=%fused_computation | loop fusion | flops 405504 | bytes 1081472 | tf_op jit(solution)/shard_map/concatenate | solution.py:26
  12.8 108.9 %shard_map.55.own_ref = f32[8,1056,128]{2,1,0:T(8,128)} custom-call(f32[1056,128]{1,0:T(8,128)} %maximum_maximum_fusion.x_ref), custom_call_target="tpu_custom_call" | custom-call | bytes 8650752 | tf_op jit(solution)/shard_map/pallas_call | solution.py:79
  121.7 0.8 slice_convert_fusion.1
  122.5 0.7 reshape.10.own_meta
  123.1 25.7 %all-gather.3.cloned.1.call-done = f32[33024,128]{1,0:T(8,128)} async-done(((f32[1032,128]{1,0:T(8,128)}), f32[33024,128]{1,0:T(8,128)}) %all-gather.3.cloned.1.call-update) | async-done | bytes 16908304 | tf_op jit(solution)/shard_map/all_gather | solution.py:166
  148.8 0.9 slice_convert_fusion
  149.7 0.7 reshape.11.far_meta
  150.4 34.6 %shard_map.56 = f32[256,1024]{1,0:T(8,128)} custom-call(s32[192]{0:T(256)} %reshape.10.own_meta, s32[768]{0:T(1024)} %reshape.11.far_meta, f32[8,1056,128]{2,1,0:T(8,128)} %shard_map.55.own_ref, f32[32,1032,128]{2,1,0:T(8,128)} %bitcast.8), custom_call_target="tpu_custom_call" | custom-call | tf_op jit(solution)/shard_map/pallas_call | solution.py:191
  (2 shorter events, 0.0 us)
Async XLA Ops:
  6.5 142.3 %all-gather.3.cloned.1.call-start = ((), (), s32[]{:S(2)}) async-start(), calls=%async_computation | async-start | bytes 17436672 | tf_op jit(solution)/shard_map/all_gather | solution.py:166
  9.1 0.7 collective-permute-start
  9.8 0.8 copy-start
Sparse Core Ops, SparseCore 0:
  10.8 138.0 all-gather.2

commit v4 on v3

--- a/solution.py
+++ b/solution.py
@@ -12,6 +12,7 @@
 CB_DEV = 16
 META = 8
 MESH = pl.DeviceIdType.MESH
+ROW_AXES = ("y", "x", "c")
 
 
 def pack(tiles, tile_rows, tile_cols, counts, scaling=None):
@@ -31,13 +32,13 @@
 
 
 def ring_kernel(n, half, x_ref, out_ref, local_sem, send_sem, recv_sem):
-    me = lax.axis_index("cols")
-    row = lax.axis_index("rows")
+    me = lax.axis_index("z")
+    here = tuple(lax.axis_index(a) for a in ROW_AXES)
     right = lax.rem(me + 1, n)
     left = lax.rem(me + n - 1, n)
     barrier = pltpu.get_barrier_semaphore()
     for neighbour in (left, right):
-        pl.semaphore_signal(barrier, inc=1, device_id=(row, neighbour), device_id_type=MESH)
+        pl.semaphore_signal(barrier, inc=1, device_id=here + (neighbour,), device_id_type=MESH)
     pl.semaphore_wait(barrier, 2)
 
     local = pltpu.make_async_copy(x_ref, out_ref.at[me], local_sem)
@@ -61,7 +62,7 @@
                 dst_ref=out_ref.at[origin, halves[way]],
                 send_sem=send_sem.at[way, step],
                 recv_sem=recv_sem.at[way, step],
-                device_id=(row, targets[way]),
+                device_id=here + (targets[way],),
                 device_id_type=MESH,
             )
             copy.start()
@@ -147,8 +148,8 @@
 
 
 def per_device(tiles, tile_rows, tile_cols, counts, scaling):
-    n_rows = lax.axis_size("rows")
-    n_cols = lax.axis_size("cols")
+    n_rows = lax.axis_size(ROW_AXES)
+    n_cols = lax.axis_size("z")
     slots = tiles.shape[1]
     far_per = n_rows // n_cols
     packed = pack(tiles, tile_rows, tile_cols, counts)
@@ -162,8 +163,10 @@
             dst_r = gp * far_per + q % far_per
             dst_c = q // far_per
             perm.append((q * n_cols + gp, dst_r * n_cols + dst_c))
-    moved = lax.ppermute(packed, ("rows", "cols"), perm)
-    far = lax.all_gather(moved[None], "rows", axis=0, tiled=True)
+    moved = lax.ppermute(packed, ROW_AXES + ("z",), perm)
+    far = lax.all_gather(moved[None], ("y", "x"), axis=0, tiled=True)
+    far = lax.all_gather(far, "c", axis=1, tiled=False)
+    far = far.reshape((n_rows,) + moved.shape)
     own = ring_gather(own_packed, n_cols)
 
     own_meta = unpack_meta(own, slots)
@@ -197,13 +200,15 @@
 
 
 def solution(mesh):
+    n_rows, n_cols = mesh.devices.shape
+    split_mesh = jax.sharding.Mesh(mesh.devices.reshape(n_rows // 8, 4, 2, n_cols), ROW_AXES + ("z",))
     placed = (
-        P("rows", "cols", None, None),
-        P("rows", "cols"),
-        P("rows", "cols"),
-        P("rows", "cols"),
-        P("cols"),
+        P(ROW_AXES, "z", None, None),
+        P(ROW_AXES, "z"),
+        P(ROW_AXES, "z"),
+        P(ROW_AXES, "z"),
+        P("z"),
     )
     return jax.shard_map(
-        per_device, mesh=mesh, in_specs=placed, out_specs=P("rows", "cols"), check_vma=False
+        per_device, mesh=split_mesh, in_specs=placed, out_specs=P(ROW_AXES, "z"), check_vma=False
     )

time: 192 us -> 248 us (1.29)
  the two profiles are of different devices: /device:TPU:1 before, /device:TPU:8 now
where the time goes in v4:
time: 248 us
  waiting for transfers between devices  131 us (53%)
  Pallas kernels  91.2 us (37%)
  between operations  14.1 us (6%)
  starting transfers between devices  5.11 us (2%)
  other arithmetic  4.5 us (2%)
    all_gather x1, waiting for transfers between devices, per_device(): far = lax.all_gather(moved[None], ('y', 'x'), axis=0, tiled=True)  93.7 us
    pallas_call x1, Pallas kernels, ring_gather(): pl.pallas_call(functools.partial(ring_kernel, n, rows // 2), out_shape=ja...  56 us
    ppermute x1, waiting for transfers between devices, per_device(): moved = lax.ppermute(packed, ROW_AXES + ('z',), perm)  37 us
    pallas_call x1, Pallas kernels, per_device(): pl.pallas_call(functools.partial(normal_kernel, slots, far_per), grid_spe...  35.2 us
    ppermute x1, starting transfers between devices, per_device(): moved = lax.ppermute(packed, ROW_AXES + ('z',), perm)  5.07 us
  transfers between devices with their start and end apart: 3, of which 2 were waited for; matrix products, arithmetic and copies ran while one was open for 1% of the time, Pallas kernels for 23%

profile of v4, /device:TPU:8, one launch (start us, length us, event | category | flops | bytes accessed | tf_op | source)
XLA Modules:
  0.0 247.9 jit_solution(13307102345446671663)
XLA Ops:
  6.5 0.0 copy-start
  6.5 0.0 copy-start.2
  6.5 0.0 all-gather.5.cloned.1.call-start
  7.3 0.1 pad.14.clone
  7.3 0.7 add_convert_fusion
  8.1 1.1 pad_maximum_fusion
  9.2 5.1 %collective-permute-start = (f32[1032,128]{1,0:T(8,128)S(1)}, f32[1032,128]{1,0:T(8,128)S(1)}, u32[]{:S(2)}, u32[]{:S(2)}) collective-permute-start(f32[1032,128]{1,0:T(8,128)S(1)} %pad_maximum_fusion), channel_id=1, source_target_pairs={{0,0},{1,32},{2,64},{3,96},{4,128},{5,160},{6,192},{7,224},{8,8},{... | collective-permute-start | bytes 1585160 | tf_op jit(solution)/shard_map/ppermute | solution.py:166
  14.2 37.0 %collective-permute-done = f32[1032,128]{1,0:T(8,128)S(1)} collective-permute-done((f32[1032,128]{1,0:T(8,128)S(1)}, f32[1032,128]{1,0:T(8,128)S(1)}, u32[]{:S(2)}, u32[]{:S(2)}) %collective-permute-start) | collective-permute-done | bytes 528416 | tf_op jit(solution)/shard_map/ppermute | solution.py:166
  51.2 0.0 copy-start.1
  51.2 0.8 copy-done.1
  52.0 0.0 all-gather.5.cloned.1.call-update
  52.0 0.0 all-gather.7.cloned.1.call-start
  52.1 93.7 %all-gather.5.cloned.1.call-done = f32[16512,128]{1,0:T(8,128)} async-done(((f32[1032,128]{1,0:T(8,128)}), f32[16512,128]{1,0:T(8,128)}) %all-gather.5.cloned.1.call-update) | async-done | bytes 8454160 | tf_op jit(solution)/shard_map/all_gather | solution.py:167
  145.7 0.0 all-gather.7.cloned.1.call-update
  145.8 0.1 pad.11.clone
  145.9 0.0 copy-done
  145.9 0.0 copy-done.2
  145.9 1.0 maximum_maximum_fusion.x_ref
  146.9 56.0 %shard_map.55.own_ref = f32[8,1056,128]{2,1,0:T(8,128)} custom-call(f32[1056,128]{1,0:T(8,128)} %maximum_maximum_fusion.x_ref), custom_call_target="tpu_custom_call" | custom-call | bytes 8650752 | tf_op jit(solution)/shard_map/pallas_call | solution.py:80
  202.9 0.8 slice_convert_fusion.1
  203.6 0.7 reshape.13.own_meta
  204.3 0.0 all-gather.7.cloned.1.call-done
  204.3 0.9 slice_convert_fusion
  205.2 0.7 reshape.15.far_meta
  205.9 35.2 %shard_map.56 = f32[256,1024]{1,0:T(8,128)} custom-call(s32[192]{0:T(256)} %reshape.13.own_meta, s32[768]{0:T(1024)} %reshape.15.far_meta, f32[8,1056,128]{2,1,0:T(8,128)} %shard_map.55.own_ref, f32[32,1032,128]{2,1,0:T(8,128)} %bitcast.9), custom_call_target="tpu_custom_call" | custom-call | tf_op jit(solution)/shard_map/pallas_call | solution.py:194
  (2 shorter events, 0.0 us)
Async XLA Ops:
  6.5 139.3 %copy-start = (f32[1,8,128,128]{3,2,1,0:T(8,128)S(1)}, f32[1,8,128,128]{3,2,1,0:T(8,128)}, u32[]{:S(2)}) copy-start(f32[1,8,128,128]{3,2,1,0:T(8,128)} %param.5) | copy-start | bytes 1572868
  6.5 139.3 %copy-start.2 = (f32[2048]{0:T(1024)S(1)}, f32[2048]{0:T(1024)}, u32[]{:S(2)}) copy-start(f32[2048]{0:T(1024)} %param.9) | copy-start | bytes 24580
  6.5 139.2 %all-gather.5.cloned.1.call-start = ((), (), s32[]{:S(2)}) async-start(), calls=%async_computation | async-start | bytes 8982528 | tf_op jit(solution)/shard_map/all_gather | solution.py:167
  9.2 42.0 %collective-permute-start = (f32[1032,128]{1,0:T(8,128)S(1)}, f32[1032,128]{1,0:T(8,128)S(1)}, u32[]{:S(2)}, u32[]{:S(2)}) collective-permute-start(f32[1032,128]{1,0:T(8,128)S(1)} %pad_maximum_fusion), channel_id=1, source_target_pairs={{0,0},{1,32},{2,64},{3,96},{4,128},{5,160},{6,192},{7,224},{8,8},{... | collective-permute-start | bytes 1585160 | tf_op jit(solution)/shard_map/ppermute | solution.py:166
  51.2 0.8 copy-start.1
  52.0 152.3 %all-gather.7.cloned.1.call-start = ((), (), s32[]{:S(2)}) async-start(), calls=%async_computation.1 | async-start | bytes 25362432 | tf_op jit(solution)/shard_map/all_gather | solution.py:168
Sparse Core Ops, SparseCore 0:
  52.1 93.5 all-gather.4
  147.6 36.1 all-gather.6

commit v5 on v3

--- a/solution.py
+++ b/solution.py
@@ -30,65 +30,148 @@
     return sets[:, slots * TB : slots * TB + 3, :slots].astype(jnp.int32).reshape(-1)
 
 
-def ring_kernel(n, half, x_ref, out_ref, local_sem, send_sem, recv_sem):
+def comm_kernel(n, side, own_half, far_half, own_x, far_x, own_out, far_out, sems, z_send, z_recv, f_send, f_recv, p_send, p_recv):
     me = lax.axis_index("cols")
     row = lax.axis_index("rows")
-    right = lax.rem(me + 1, n)
-    left = lax.rem(me + n - 1, n)
+    core = row % 2
+    y = row // (2 * side)
+    x = (row // 2) % side
+    step_a = (core, 1 - core)
+    step_b = (1 - core, core)
+
+    def spot(da, db, cc):
+        yy = (y + da * step_a[0] + db * step_b[0] + 2 * side) % side
+        xx = (x + da * step_a[1] + db * step_b[1] + 2 * side) % side
+        return (yy * side + xx) * 2 + cc
+
+    z_right = lax.rem(me + 1, n)
+    z_left = lax.rem(me + n - 1, n)
+    partner = row - core + (1 - core)
     barrier = pltpu.get_barrier_semaphore()
-    for neighbour in (left, right):
-        pl.semaphore_signal(barrier, inc=1, device_id=(row, neighbour), device_id_type=MESH)
-    pl.semaphore_wait(barrier, 2)
-
-    local = pltpu.make_async_copy(x_ref, out_ref.at[me], local_sem)
-    local.start()
-    halves = (pl.ds(0, half), pl.ds(half, half))
-    targets = (right, left)
-    previous = [None, None]
-    for step in range(n - 1):
+    peers = [(row, z_left), (row, z_right), (partner, me)]
+    for s in (1, -1):
+        peers.append((spot(s, 0, core), me))
+        peers.append((spot(0, s, core), me))
+    for peer in peers:
+        pl.semaphore_signal(barrier, inc=1, device_id=peer, device_id_type=MESH)
+    pl.semaphore_wait(barrier, len(peers))
+
+    local_own = pltpu.make_async_copy(own_x, own_out.at[me], sems.at[0])
+    local_own.start()
+    local_far = pltpu.make_async_copy(far_x, far_out.at[spot(0, 0, core)], sems.at[1])
+    local_far.start()
+
+    far_rows = far_x.shape[0]
+    halves = (pl.ds(0, far_half), pl.ds(far_half, far_rows - far_half))
+    started = []
+    partner_copies = []
+
+    def send(src, dst, sem_s, sem_r, peer):
+        copy = pltpu.make_async_remote_copy(
+            src_ref=src, dst_ref=dst, send_sem=sem_s, recv_sem=sem_r, device_id=peer, device_id_type=MESH
+        )
+        copy.start()
+        started.append(copy)
+        return copy
+
+    def to_partner(slot, src=None):
+        j = len(partner_copies)
+        src = far_out.at[slot] if src is None else src
+        partner_copies.append(send(src, far_out.at[slot], p_send.at[j], p_recv.at[j], (partner, me)))
+
+    own_halves = (pl.ds(0, own_half), pl.ds(own_half, own_half))
+    z_prev = [None, None]
+
+    def z_step(step):
+        if step >= n - 1:
+            return
         for way in range(2):
             if way == 0:
                 origin = lax.rem(me - step + n, n)
             else:
                 origin = lax.rem(me + step, n)
             if step == 0:
-                src_ref = x_ref.at[halves[way]]
+                src = own_x.at[own_halves[way]]
             else:
-                previous[way].wait_recv()
-                src_ref = out_ref.at[origin, halves[way]]
-            copy = pltpu.make_async_remote_copy(
-                src_ref=src_ref,
-                dst_ref=out_ref.at[origin, halves[way]],
-                send_sem=send_sem.at[way, step],
-                recv_sem=recv_sem.at[way, step],
-                device_id=(row, targets[way]),
-                device_id_type=MESH,
+                z_prev[way].wait_recv()
+                src = own_out.at[origin, own_halves[way]]
+            z_prev[way] = send(
+                src, own_out.at[origin, own_halves[way]], z_send.at[way, step], z_recv.at[way, step],
+                (row, (z_right, z_left)[way]),
             )
-            copy.start()
-            if previous[way] is not None:
-                previous[way].wait_send()
-            previous[way] = copy
+
+    z_step(0)
+    to_partner(spot(0, 0, core), far_x)
+    first = [send(far_x, far_out.at[spot(0, 0, core)], f_send.at[0, w], f_recv.at[0, w], (spot(s, 0, core), me))
+             for w, s in enumerate((1, -1))]
+    for copy in first:
+        copy.wait_recv()
+    to_partner(spot(-1, 0, core))
+    to_partner(spot(1, 0, core))
+    second = [send(far_out.at[spot(-s, 0, core), halves[w]], far_out.at[spot(-s, 0, core), halves[w]],
+                   f_send.at[1, w], f_recv.at[1, w], (spot(s, 0, core), me))
+              for w, s in enumerate((1, -1))]
+    z_step(1)
+    for copy in second:
+        copy.wait_recv()
+    to_partner(spot(2, 0, core))
+    held = (0, -1, 1, 2)
+    third = []
+    for w, s in enumerate((1, -1)):
+        for i, da in enumerate(held):
+            slot = spot(da, 0, core)
+            third.append(send(far_x if da == 0 else far_out.at[slot], far_out.at[slot], f_send.at[2 + w, i], f_recv.at[2 + w, i],
+                              (spot(0, s, core), me)))
+    z_step(2)
+    for copy in third:
+        copy.wait_recv()
+    for s in (1, -1):
+        for da in held:
+            to_partner(spot(da, -s, core))
+    fourth = []
+    for w, s in enumerate((1, -1)):
+        for i, da in enumerate(held):
+            slot = spot(da, -s, core)
+            fourth.append(send(far_out.at[slot, halves[w]], far_out.at[slot, halves[w]],
+                               f_send.at[4 + w, i], f_recv.at[4 + w, i], (spot(0, s, core), me)))
+    z_step(3)
+    for copy in fourth:
+        copy.wait_recv()
+    for da in held:
+        to_partner(spot(da, 2, core))
+    for step in range(4, n - 1):
+        z_step(step)
     for way in range(2):
-        previous[way].wait_recv()
-        previous[way].wait_send()
-    local.wait()
-
-
-def ring_gather(x, n):
-    rows = x.shape[0]
+        z_prev[way].wait_recv()
+    for copy in partner_copies:
+        copy.wait_recv()
+    for copy in started:
+        copy.wait_send()
+    local_own.wait()
+    local_far.wait()
+
+
+def gather_all(own_x, far_x, n, n_far):
+    side = 4
     return pl.pallas_call(
-        functools.partial(ring_kernel, n, rows // 2),
-        out_shape=jax.ShapeDtypeStruct((n,) + x.shape, x.dtype),
-        in_specs=[pl.BlockSpec(memory_space=pl.ANY)],
-        out_specs=pl.BlockSpec(memory_space=pl.ANY),
+        functools.partial(comm_kernel, n, side, own_x.shape[0] // 2, 512),
+        out_shape=(
+            jax.ShapeDtypeStruct((n,) + own_x.shape, own_x.dtype),
+            jax.ShapeDtypeStruct((n_far,) + far_x.shape, far_x.dtype),
+        ),
+        in_specs=[pl.BlockSpec(memory_space=pl.ANY)] * 2,
+        out_specs=(pl.BlockSpec(memory_space=pl.ANY), pl.BlockSpec(memory_space=pl.ANY)),
         scratch_shapes=[
-            pltpu.SemaphoreType.DMA(()),
+            pltpu.SemaphoreType.DMA((2,)),
             pltpu.SemaphoreType.DMA((2, n - 1)),
             pltpu.SemaphoreType.DMA((2, n - 1)),
+            pltpu.SemaphoreType.DMA((6, 4)),
+            pltpu.SemaphoreType.DMA((6, 4)),
+            pltpu.SemaphoreType.DMA((n_far // 2,)),
+            pltpu.SemaphoreType.DMA((n_far // 2,)),
         ],
         compiler_params=pltpu.CompilerParams(collective_id=0, has_side_effects=True),
-        cost_estimate=pl.CostEstimate(flops=0, bytes_accessed=2 * n * x.size * 4, transcendentals=0),
-    )(x)
+    )(own_x, far_x)
 
 
 def split(x):
@@ -163,8 +246,7 @@
             dst_c = q // far_per
             perm.append((q * n_cols + gp, dst_r * n_cols + dst_c))
     moved = lax.ppermute(packed, ("rows", "cols"), perm)
-    far = lax.all_gather(moved[None], "rows", axis=0, tiled=True)
-    own = ring_gather(own_packed, n_cols)
+    own, far = gather_all(own_packed, moved, n_cols, n_rows)
 
     own_meta = unpack_meta(own, slots)
     far_meta = unpack_meta(far, slots)

time: 192 us -> 186 us (0.969)
  the two profiles are of different devices: /device:TPU:1 before, /device:TPU:4 now
where the time goes in v5:
time: 186 us
  Pallas kernels  135 us (73%)
  waiting for transfers between devices  38.8 us (21%)
  other arithmetic  5.56 us (3%)
  starting transfers between devices  3.77 us (2%)
  local copies, waits for them, and re-layouts  2.33 us (1%)
    pallas_call x1, Pallas kernels, gather_all(): pl.pallas_call(functools.partial(comm_kernel, n, side, own_x.shape[0] //...  100 us
    ppermute x1, waiting for transfers between devices, per_device(): moved = lax.ppermute(packed, ('rows', 'cols'), perm)  38.8 us
    pallas_call x1, Pallas kernels, per_device(): pl.pallas_call(functools.partial(normal_kernel, slots, far_per), grid_spe...  34.7 us
    ppermute x1, starting transfers between devices, per_device(): moved = lax.ppermute(packed, ('rows', 'cols'), perm)  3.77 us
  transfers between devices with their start and end apart: 1, of which 1 were waited for; matrix products, arithmetic and copies ran while one was open for 1% of the time, Pallas kernels for 0%

profile of v5, /device:TPU:4, one launch (start us, length us, event | category | flops | bytes accessed | tf_op | source)
XLA Modules:
  0.0 186.1 jit_solution(13195267824465268807)
XLA Ops:
  0.7 0.1 pad.14.clone
  0.7 0.7 add_convert_fusion
  1.5 1.1 pad_maximum_fusion
  2.6 3.8 %collective-permute-start = (f32[1032,128]{1,0:T(8,128)S(1)}, f32[1032,128]{1,0:T(8,128)S(1)}, u32[]{:S(2)}, u32[]{:S(2)}) collective-permute-start(f32[1032,128]{1,0:T(8,128)S(1)} %pad_maximum_fusion), channel_id=1, source_target_pairs={{0,0},{1,32},{2,64},{3,96},{4,128},{5,160},{6,192},{7,224},{8,8},{... | collective-permute-start | bytes 1585160 | tf_op jit(solution)/shard_map/ppermute | solution.py:248
  6.3 0.1 pad.11.clone
  6.4 2.1 %maximum_maximum_fusion.own_x = f32[1056,128]{1,0:T(8,128)} fusion(f32[16,128]{1,0:T(8,128)} %bitcast.8, f32[8,128]{1,0:T(8,128)S(1)} %pad.5, f32[1024,128]{1,0:T(8,128)} %bitcast.7, f32[1056]{0:T(1024)S(1)} %pad.11.clone), kind=kLoop, calls=%fused_computation | loop fusion | flops 405504 | bytes 1081472 | tf_op jit(solution)/shard_map/concatenate | solution.py:26
  8.5 38.8 %collective-permute-done.far_x = f32[1032,128]{1,0:T(8,128)S(1)} collective-permute-done((f32[1032,128]{1,0:T(8,128)S(1)}, f32[1032,128]{1,0:T(8,128)S(1)}, u32[]{:S(2)}, u32[]{:S(2)}) %collective-permute-start) | collective-permute-done | bytes 528416 | tf_op jit(solution)/shard_map/ppermute | solution.py:248
  47.3 0.0 copy-start
  47.3 0.8 copy-done
  48.1 100.2 %shard_map.55 = (f32[8,1056,128]{2,1,0:T(8,128)}, f32[32,1032,128]{2,1,0:T(8,128)}) custom-call(f32[1056,128]{1,0:T(8,128)} %maximum_maximum_fusion.own_x, f32[1032,128]{1,0:T(8,128)} %copy-done), custom_call_target="tpu_custom_call" | custom-call | tf_op jit(solution)/shard_map/pallas_call | solution.py:156
  148.3 0.8 slice_convert_fusion.1
  149.1 0.7 reshape.10.own_meta
  149.7 0.9 slice_convert_fusion
  150.6 0.7 reshape.11.far_meta
  151.3 34.7 %shard_map.56 = f32[256,1024]{1,0:T(8,128)} custom-call(s32[192]{0:T(256)} %reshape.10.own_meta, s32[768]{0:T(1024)} %reshape.11.far_meta, f32[8,1056,128]{2,1,0:T(8,128)} %get-tuple-element.7.own_ref, f32[32,1032,128]{2,1,0:T(8,128)} %get-tuple-element.8.far_ref), custom_call_target="tpu_custom_call" | custom-call | tf_op jit(solution)/shard_map/pallas_call | solution.py:273
  (2 shorter events, 0.0 us)
Async XLA Ops:
  2.6 44.7 %collective-permute-start = (f32[1032,128]{1,0:T(8,128)S(1)}, f32[1032,128]{1,0:T(8,128)S(1)}, u32[]{:S(2)}, u32[]{:S(2)}) collective-permute-start(f32[1032,128]{1,0:T(8,128)S(1)} %pad_maximum_fusion), channel_id=1, source_target_pairs={{0,0},{1,32},{2,64},{3,96},{4,128},{5,160},{6,192},{7,224},{8,8},{... | collective-permute-start | bytes 1585160 | tf_op jit(solution)/shard_map/ppermute | solution.py:248
  47.3 0.8 copy-start

commit v6 on v5

--- a/solution.py
+++ b/solution.py
@@ -47,8 +47,12 @@
     z_right = lax.rem(me + 1, n)
     z_left = lax.rem(me + n - 1, n)
     partner = row - core + (1 - core)
+    far_per = far_out.shape[0] // n
+    dest = (lax.rem(me + 1, n) * far_per + row % far_per, row // far_per)
+    origin_plane = lax.rem(row // far_per + n - 1, n)
+    source = (me * far_per + row % far_per, origin_plane)
     barrier = pltpu.get_barrier_semaphore()
-    peers = [(row, z_left), (row, z_right), (partner, me)]
+    peers = [(row, z_left), (row, z_right), (partner, me), dest, source]
     for s in (1, -1):
         peers.append((spot(s, 0, core), me))
         peers.append((spot(0, s, core), me))
@@ -58,8 +62,6 @@
 
     local_own = pltpu.make_async_copy(own_x, own_out.at[me], sems.at[0])
     local_own.start()
-    local_far = pltpu.make_async_copy(far_x, far_out.at[spot(0, 0, core)], sems.at[1])
-    local_far.start()
 
     far_rows = far_x.shape[0]
     halves = (pl.ds(0, far_half), pl.ds(far_half, far_rows - far_half))
@@ -101,8 +103,10 @@
             )
 
     z_step(0)
-    to_partner(spot(0, 0, core), far_x)
-    first = [send(far_x, far_out.at[spot(0, 0, core)], f_send.at[0, w], f_recv.at[0, w], (spot(s, 0, core), me))
+    moved = send(far_x, far_out.at[dest[0]], sems.at[1], sems.at[2], dest)
+    moved.wait_recv()
+    to_partner(spot(0, 0, core))
+    first = [send(far_out.at[spot(0, 0, core)], far_out.at[spot(0, 0, core)], f_send.at[0, w], f_recv.at[0, w], (spot(s, 0, core), me))
              for w, s in enumerate((1, -1))]
     for copy in first:
         copy.wait_recv()
@@ -120,7 +124,7 @@
     for w, s in enumerate((1, -1)):
         for i, da in enumerate(held):
             slot = spot(da, 0, core)
-            third.append(send(far_x if da == 0 else far_out.at[slot], far_out.at[slot], f_send.at[2 + w, i], f_recv.at[2 + w, i],
+            third.append(send(far_out.at[slot], far_out.at[slot], f_send.at[2 + w, i], f_recv.at[2 + w, i],
                               (spot(0, s, core), me)))
     z_step(2)
     for copy in third:
@@ -148,7 +152,6 @@
     for copy in started:
         copy.wait_send()
     local_own.wait()
-    local_far.wait()
 
 
 def gather_all(own_x, far_x, n, n_far):
@@ -162,7 +165,7 @@
         in_specs=[pl.BlockSpec(memory_space=pl.ANY)] * 2,
         out_specs=(pl.BlockSpec(memory_space=pl.ANY), pl.BlockSpec(memory_space=pl.ANY)),
         scratch_shapes=[
-            pltpu.SemaphoreType.DMA((2,)),
+            pltpu.SemaphoreType.DMA((3,)),
             pltpu.SemaphoreType.DMA((2, n - 1)),
             pltpu.SemaphoreType.DMA((2, n - 1)),
             pltpu.SemaphoreType.DMA((6, 4)),
@@ -184,7 +187,7 @@
     return lax.dot_general(a, b, (((1,), (1,)), ((), ())), preferred_element_type=jnp.float32)
 
 
-def normal_kernel(slots, far_per, own_meta, far_meta, own_ref, far_ref, out_ref, dense, p_hi, p_lo, x_hi, x_lo, z_hi, z_lo):
+def normal_kernel(slots, far_per, n_groups, own_meta, far_meta, own_ref, far_ref, out_ref, dense, p_hi, p_lo, x_hi, x_lo, z_hi, z_lo):
     g = pl.program_id(0)
 
     @pl.when(g == 0)
@@ -209,7 +212,7 @@
     p_lo[...] = lo
 
     for qi in range(far_per):
-        base = (g * far_per + qi) * 3 * slots
+        base = (lax.rem(g + 1, n_groups) * far_per + qi) * 3 * slots
         count = far_meta[base + 2 * slots]
         for k in range(slots):
             r = far_meta[base + k]
@@ -239,14 +242,7 @@
     own_packed = pack(tiles, tile_rows, tile_cols, counts, scaling)
     own_len = own_packed.shape[0]
 
-    perm = []
-    for q in range(n_rows):
-        for gp in range(n_cols):
-            dst_r = gp * far_per + q % far_per
-            dst_c = q // far_per
-            perm.append((q * n_cols + gp, dst_r * n_cols + dst_c))
-    moved = lax.ppermute(packed, ("rows", "cols"), perm)
-    own, far = gather_all(own_packed, moved, n_cols, n_rows)
+    own, far = gather_all(own_packed, packed, n_cols, n_rows)
 
     own_meta = unpack_meta(own, slots)
     far_meta = unpack_meta(far, slots)
@@ -257,7 +253,7 @@
         grid=(n_cols,),
         in_specs=[
             pl.BlockSpec((1, own_len, TB), lambda g, om, fm: (g, 0, 0)),
-            pl.BlockSpec((far_per, set_len, TB), lambda g, om, fm: (g, 0, 0)),
+            pl.BlockSpec((far_per, set_len, TB), lambda g, om, fm: ((g + 1) % n_cols, 0, 0)),
         ],
         out_specs=pl.BlockSpec((RB * TB, out_cols), lambda g, om, fm: (0, 0)),
         scratch_shapes=[
@@ -271,7 +267,7 @@
         ],
     )
     return pl.pallas_call(
-        functools.partial(normal_kernel, slots, far_per),
+        functools.partial(normal_kernel, slots, far_per, n_cols),
         grid_spec=grid_spec,
         out_shape=jax.ShapeDtypeStruct((RB * TB, out_cols), jnp.float32),
         compiler_params=pltpu.CompilerParams(dimension_semantics=("arbitrary",)),

time: 186 us -> 188 us (1.011)
  the two profiles are of different devices: /device:TPU:4 before, /device:TPU:32 now
where the time goes in v6:
time: 188 us
  Pallas kernels  179 us (95%)
  other arithmetic  6.36 us (3%)
    pallas_call x1, Pallas kernels, gather_all(): pl.pallas_call(functools.partial(comm_kernel, n, side, own_x.shape[0] //...  145 us
    pallas_call x1, Pallas kernels, per_device(): pl.pallas_call(functools.partial(normal_kernel, slots, far_per, n_cols),...  34.6 us
    concatenate x2, other arithmetic, pack(): return jnp.concatenate(parts, axis=0)  3.94 us

profile of v6, /device:TPU:32, one launch (start us, length us, event | category | flops | bytes accessed | tf_op | source)
XLA Modules:
  0.0 188.0 jit_solution(14707816354825897841)
XLA Ops:
  0.7 0.1 pad.14.clone
  0.7 0.7 add_convert_fusion
  1.5 0.1 pad.11.clone
  1.6 1.9 pad_maximum_fusion.far_x
  3.4 2.1 %maximum_maximum_fusion.own_x = f32[1056,128]{1,0:T(8,128)} fusion(f32[16,128]{1,0:T(8,128)} %bitcast.8, f32[8,128]{1,0:T(8,128)S(1)} %pad.5, f32[1024,128]{1,0:T(8,128)} %bitcast.7, f32[1056]{0:T(1024)S(1)} %pad.11.clone), kind=kLoop, calls=%fused_computation | loop fusion | flops 405504 | bytes 1081472 | tf_op jit(solution)/shard_map/concatenate | solution.py:26
  5.5 144.8 %shard_map.55 = (f32[8,1056,128]{2,1,0:T(8,128)}, f32[32,1032,128]{2,1,0:T(8,128)}) custom-call(f32[1056,128]{1,0:T(8,128)} %maximum_maximum_fusion.own_x, f32[1032,128]{1,0:T(8,128)} %pad_maximum_fusion.far_x), custom_call_target="tpu_custom_call" | custom-call | tf_op jit(solution)/shard_map/pallas_call | solution.py:159
  150.3 0.8 slice_convert_fusion.1
  151.1 0.6 reshape.10.own_meta
  151.7 0.9 slice_convert_fusion
  152.6 0.7 reshape.11.far_meta
  153.3 34.6 %shard_map.56 = f32[256,1024]{1,0:T(8,128)} custom-call(s32[192]{0:T(256)} %reshape.10.own_meta, s32[768]{0:T(1024)} %reshape.11.far_meta, f32[8,1056,128]{2,1,0:T(8,128)} %get-tuple-element.7.own_ref, f32[32,1032,128]{2,1,0:T(8,128)} %get-tuple-element.8.far_ref), custom_call_target="tpu_custom_call" | custom-call | tf_op jit(solution)/shard_map/pallas_call | solution.py:269
  (2 shorter events, 0.0 us)

commit v7 on v6

--- a/solution.py
+++ b/solution.py
@@ -104,6 +104,8 @@
 
     z_step(0)
     moved = send(far_x, far_out.at[dest[0]], sems.at[1], sems.at[2], dest)
+    for step in range(1, 5):
+        z_step(step)
     moved.wait_recv()
     to_partner(spot(0, 0, core))
     first = [send(far_out.at[spot(0, 0, core)], far_out.at[spot(0, 0, core)], f_send.at[0, w], f_recv.at[0, w], (spot(s, 0, core), me))
@@ -115,7 +117,7 @@
     second = [send(far_out.at[spot(-s, 0, core), halves[w]], far_out.at[spot(-s, 0, core), halves[w]],
                    f_send.at[1, w], f_recv.at[1, w], (spot(s, 0, core), me))
               for w, s in enumerate((1, -1))]
-    z_step(1)
+    z_step(5)
     for copy in second:
         copy.wait_recv()
     to_partner(spot(2, 0, core))
@@ -126,7 +128,7 @@
             slot = spot(da, 0, core)
             third.append(send(far_out.at[slot], far_out.at[slot], f_send.at[2 + w, i], f_recv.at[2 + w, i],
                               (spot(0, s, core), me)))
-    z_step(2)
+    z_step(6)
     for copy in third:
         copy.wait_recv()
     for s in (1, -1):
@@ -138,12 +140,11 @@
             slot = spot(da, -s, core)
             fourth.append(send(far_out.at[slot, halves[w]], far_out.at[slot, halves[w]],
                                f_send.at[4 + w, i], f_recv.at[4 + w, i], (spot(0, s, core), me)))
-    z_step(3)
     for copy in fourth:
         copy.wait_recv()
     for da in held:
         to_partner(spot(da, 2, core))
-    for step in range(4, n - 1):
+    for step in range(7, n - 1):
         z_step(step)
     for way in range(2):
         z_prev[way].wait_recv()

time: 188 us -> 192 us (1.021)
  the two profiles are of different devices: /device:TPU:32 before, /device:TPU:1 now
where the time goes in v7:
time: 192 us; the launch traced here: 191 us
  Pallas kernels  183 us (95%)
  other arithmetic  6.36 us (3%)
    pallas_call x1, Pallas kernels, gather_all(): pl.pallas_call(functools.partial(comm_kernel, n, side, own_x.shape[0] //...  148 us
    pallas_call x1, Pallas kernels, per_device(): pl.pallas_call(functools.partial(normal_kernel, slots, far_per, n_cols),...  34.7 us
    concatenate x2, other arithmetic, pack(): return jnp.concatenate(parts, axis=0)  3.94 us

profile of v7, /device:TPU:1, one launch (start us, length us, event | category | flops | bytes accessed | tf_op | source)
XLA Modules:
  0.0 191.5 jit_solution(16311183024698782946)
XLA Ops:
  0.7 0.1 pad.14.clone
  0.7 0.7 add_convert_fusion
  1.5 0.1 pad.11.clone
  1.6 1.9 pad_maximum_fusion.far_x
  3.4 2.1 %maximum_maximum_fusion.own_x = f32[1056,128]{1,0:T(8,128)} fusion(f32[16,128]{1,0:T(8,128)} %bitcast.8, f32[8,128]{1,0:T(8,128)S(1)} %pad.5, f32[1024,128]{1,0:T(8,128)} %bitcast.7, f32[1056]{0:T(1024)S(1)} %pad.11.clone), kind=kLoop, calls=%fused_computation | loop fusion | flops 405504 | bytes 1081472 | tf_op jit(solution)/shard_map/concatenate | solution.py:26
  5.5 148.2 %shard_map.55 = (f32[8,1056,128]{2,1,0:T(8,128)}, f32[32,1032,128]{2,1,0:T(8,128)}) custom-call(f32[1056,128]{1,0:T(8,128)} %maximum_maximum_fusion.own_x, f32[1032,128]{1,0:T(8,128)} %pad_maximum_fusion.far_x), custom_call_target="tpu_custom_call" | custom-call | tf_op jit(solution)/shard_map/pallas_call | solution.py:160
  153.7 0.8 slice_convert_fusion.1
  154.5 0.6 reshape.10.own_meta
  155.1 0.9 slice_convert_fusion
  156.0 0.7 reshape.11.far_meta
  156.7 34.7 %shard_map.56 = f32[256,1024]{1,0:T(8,128)} custom-call(s32[192]{0:T(256)} %reshape.10.own_meta, s32[768]{0:T(1024)} %reshape.11.far_meta, f32[8,1056,128]{2,1,0:T(8,128)} %get-tuple-element.7.own_ref, f32[32,1032,128]{2,1,0:T(8,128)} %get-tuple-element.8.far_ref), custom_call_target="tpu_custom_call" | custom-call | tf_op jit(solution)/shard_map/pallas_call | solution.py:270
  (2 shorter events, 0.0 us)

commit v8 on v6

--- a/solution.py
+++ b/solution.py
@@ -30,7 +30,7 @@
     return sets[:, slots * TB : slots * TB + 3, :slots].astype(jnp.int32).reshape(-1)
 
 
-def comm_kernel(n, side, own_half, far_half, own_x, far_x, own_out, far_out, sems, z_send, z_recv, f_send, f_recv, p_send, p_recv):
+def comm_kernel(n, side, own_half, far_half, own_x, far_x, own_out, far_out, sems, perm_send, perm_recv, z_send, z_recv, f_send, f_recv, p_send, p_recv):
     me = lax.axis_index("cols")
     row = lax.axis_index("rows")
     core = row % 2
@@ -64,8 +64,16 @@
     local_own.start()
 
     far_rows = far_x.shape[0]
-    halves = (pl.ds(0, far_half), pl.ds(far_half, far_rows - far_half))
+    cut = far_half
+    chunks = (pl.ds(0, cut), pl.ds(cut, far_rows - cut))
+    first_half = (cut // 2) // META * META
+    second_half = ((far_rows - cut) // 2) // META * META
+    halves = (
+        (pl.ds(0, first_half), pl.ds(first_half, cut - first_half)),
+        (pl.ds(cut, second_half), pl.ds(cut + second_half, far_rows - cut - second_half)),
+    )
     started = []
+    partner_count = [0, 0]
     partner_copies = []
 
     def send(src, dst, sem_s, sem_r, peer):
@@ -76,10 +84,11 @@
         started.append(copy)
         return copy
 
-    def to_partner(slot, src=None):
-        j = len(partner_copies)
-        src = far_out.at[slot] if src is None else src
-        partner_copies.append(send(src, far_out.at[slot], p_send.at[j], p_recv.at[j], (partner, me)))
+    def to_partner(h, slot):
+        j = partner_count[h]
+        partner_count[h] += 1
+        ref = far_out.at[slot, chunks[h]]
+        partner_copies.append(send(ref, ref, p_send.at[h, j], p_recv.at[h, j], (partner, me)))
 
     own_halves = (pl.ds(0, own_half), pl.ds(own_half, own_half))
     z_prev = [None, None]
@@ -102,48 +111,77 @@
                 (row, (z_right, z_left)[way]),
             )
 
+    held = (0, -1, 1, 2)
+
+    def far_stages(h):
+        box = {}
+        rows = chunks[h]
+
+        def s0():
+            box["moved"] = send(far_x.at[rows], far_out.at[dest[0], rows], perm_send.at[h], perm_recv.at[h], dest)
+
+        def s1():
+            box["moved"].wait_recv()
+            to_partner(h, spot(0, 0, core))
+            box["first"] = [
+                send(far_out.at[spot(0, 0, core), rows], far_out.at[spot(0, 0, core), rows],
+                     f_send.at[h, 0, w], f_recv.at[h, 0, w], (spot(s, 0, core), me))
+                for w, s in enumerate((1, -1))
+            ]
+
+        def s2():
+            for copy in box["first"]:
+                copy.wait_recv()
+            to_partner(h, spot(-1, 0, core))
+            to_partner(h, spot(1, 0, core))
+            box["second"] = [
+                send(far_out.at[spot(-s, 0, core), halves[h][w]], far_out.at[spot(-s, 0, core), halves[h][w]],
+                     f_send.at[h, 1, w], f_recv.at[h, 1, w], (spot(s, 0, core), me))
+                for w, s in enumerate((1, -1))
+            ]
+
+        def s3():
+            for copy in box["second"]:
+                copy.wait_recv()
+            to_partner(h, spot(2, 0, core))
+            box["third"] = []
+            for w, s in enumerate((1, -1)):
+                for i, da in enumerate(held):
+                    slot = spot(da, 0, core)
+                    box["third"].append(send(far_out.at[slot, rows], far_out.at[slot, rows],
+                                             f_send.at[h, 2 + w, i], f_recv.at[h, 2 + w, i], (spot(0, s, core), me)))
+
+        def s4():
+            for copy in box["third"]:
+                copy.wait_recv()
+            for s in (1, -1):
+                for da in held:
+                    to_partner(h, spot(da, -s, core))
+            box["fourth"] = []
+            for w, s in enumerate((1, -1)):
+                for i, da in enumerate(held):
+                    slot = spot(da, -s, core)
+                    box["fourth"].append(send(far_out.at[slot, halves[h][w]], far_out.at[slot, halves[h][w]],
+                                              f_send.at[h, 4 + w, i], f_recv.at[h, 4 + w, i], (spot(0, s, core), me)))
+
+        def s5():
+            for copy in box["fourth"]:
+                copy.wait_recv()
+            for da in held:
+                to_partner(h, spot(da, 2, core))
+
+        return [s0, s1, s2, s3, s4, s5]
+
+    lead = far_stages(0)
+    lag = far_stages(1)
     z_step(0)
-    moved = send(far_x, far_out.at[dest[0]], sems.at[1], sems.at[2], dest)
-    moved.wait_recv()
-    to_partner(spot(0, 0, core))
-    first = [send(far_out.at[spot(0, 0, core)], far_out.at[spot(0, 0, core)], f_send.at[0, w], f_recv.at[0, w], (spot(s, 0, core), me))
-             for w, s in enumerate((1, -1))]
-    for copy in first:
-        copy.wait_recv()
-    to_partner(spot(-1, 0, core))
-    to_partner(spot(1, 0, core))
-    second = [send(far_out.at[spot(-s, 0, core), halves[w]], far_out.at[spot(-s, 0, core), halves[w]],
-                   f_send.at[1, w], f_recv.at[1, w], (spot(s, 0, core), me))
-              for w, s in enumerate((1, -1))]
-    z_step(1)
-    for copy in second:
-        copy.wait_recv()
-    to_partner(spot(2, 0, core))
-    held = (0, -1, 1, 2)
-    third = []
-    for w, s in enumerate((1, -1)):
-        for i, da in enumerate(held):
-            slot = spot(da, 0, core)
-            third.append(send(far_out.at[slot], far_out.at[slot], f_send.at[2 + w, i], f_recv.at[2 + w, i],
-                              (spot(0, s, core), me)))
-    z_step(2)
-    for copy in third:
-        copy.wait_recv()
-    for s in (1, -1):
-        for da in held:
-            to_partner(spot(da, -s, core))
-    fourth = []
-    for w, s in enumerate((1, -1)):
-        for i, da in enumerate(held):
-            slot = spot(da, -s, core)
-            fourth.append(send(far_out.at[slot, halves[w]], far_out.at[slot, halves[w]],
-                               f_send.at[4 + w, i], f_recv.at[4 + w, i], (spot(0, s, core), me)))
-    z_step(3)
-    for copy in fourth:
-        copy.wait_recv()
-    for da in held:
-        to_partner(spot(da, 2, core))
-    for step in range(4, n - 1):
+    lead[0]()
+    for tick in range(1, len(lead) + 1):
+        if tick < len(lead):
+            lead[tick]()
+        lag[tick - 1]()
+        z_step(tick)
+    for step in range(len(lead) + 1, n - 1):
         z_step(step)
     for way in range(2):
         z_prev[way].wait_recv()
@@ -165,13 +203,15 @@
         in_specs=[pl.BlockSpec(memory_space=pl.ANY)] * 2,
         out_specs=(pl.BlockSpec(memory_space=pl.ANY), pl.BlockSpec(memory_space=pl.ANY)),
         scratch_shapes=[
-            pltpu.SemaphoreType.DMA((3,)),
+            pltpu.SemaphoreType.DMA((1,)),
+            pltpu.SemaphoreType.DMA((2,)),
+            pltpu.SemaphoreType.DMA((2,)),
             pltpu.SemaphoreType.DMA((2, n - 1)),
             pltpu.SemaphoreType.DMA((2, n - 1)),
-            pltpu.SemaphoreType.DMA((6, 4)),
-            pltpu.SemaphoreType.DMA((6, 4)),
-            pltpu.SemaphoreType.DMA((n_far // 2,)),
-            pltpu.SemaphoreType.DMA((n_far // 2,)),
+            pltpu.SemaphoreType.DMA((2, 6, 4)),
+            pltpu.SemaphoreType.DMA((2, 6, 4)),
+            pltpu.SemaphoreType.DMA((2, n_far // 2)),
+            pltpu.SemaphoreType.DMA((2, n_far // 2)),
         ],
         compiler_params=pltpu.CompilerParams(collective_id=0, has_side_effects=True),
     )(own_x, far_x)

time: 188 us -> 167 us (0.89)
  the two profiles are of different devices: /device:TPU:32 before, /device:TPU:1 now
where the time goes in v8:
time: 167 us
  Pallas kernels  159 us (95%)
  other arithmetic  6.36 us (4%)
    pallas_call x1, Pallas kernels, gather_all(): pl.pallas_call(functools.partial(comm_kernel, n, side, own_x.shape[0] //...  124 us
    pallas_call x1, Pallas kernels, per_device(): pl.pallas_call(functools.partial(normal_kernel, slots, far_per, n_cols),...  34.8 us
    concatenate x2, other arithmetic, pack(): return jnp.concatenate(parts, axis=0)  3.94 us

profile of v8, /device:TPU:1, one launch (start us, length us, event | category | flops | bytes accessed | tf_op | source)
XLA Modules:
  0.0 167.2 jit_solution(16058976691548696218)
XLA Ops:
  0.7 0.1 pad.14.clone
  0.7 0.7 add_convert_fusion
  1.5 0.1 pad.11.clone
  1.6 1.9 %pad_maximum_fusion.far_x = f32[1032,128]{1,0:T(8,128)} fusion(f32[8,128]{1,0:T(8,128)S(1)} %pad.5, f32[1024,128]{1,0:T(8,128)} %bitcast.6), kind=kLoop, calls=%fused_computation.1 | loop fusion | flops 132096 | bytes 1056768 | tf_op jit(solution)/shard_map/concatenate | solution.py:26
  3.4 2.1 %maximum_maximum_fusion.own_x = f32[1056,128]{1,0:T(8,128)} fusion(f32[16,128]{1,0:T(8,128)} %bitcast.8, f32[8,128]{1,0:T(8,128)S(1)} %pad.5, f32[1024,128]{1,0:T(8,128)} %bitcast.7, f32[1056]{0:T(1024)S(1)} %pad.11.clone), kind=kLoop, calls=%fused_computation | loop fusion | flops 405504 | bytes 1081472 | tf_op jit(solution)/shard_map/concatenate | solution.py:26
  5.5 123.9 %shard_map.55 = (f32[8,1056,128]{2,1,0:T(8,128)}, f32[32,1032,128]{2,1,0:T(8,128)}) custom-call(f32[1056,128]{1,0:T(8,128)} %maximum_maximum_fusion.own_x, f32[1032,128]{1,0:T(8,128)} %pad_maximum_fusion.far_x), custom_call_target="tpu_custom_call" | custom-call | tf_op jit(solution)/shard_map/pallas_call | solution.py:197
  129.4 0.8 slice_convert_fusion.1
  130.1 0.6 reshape.10.own_meta
  130.8 0.9 slice_convert_fusion
  131.7 0.7 reshape.11.far_meta
  132.4 34.8 %shard_map.56 = f32[256,1024]{1,0:T(8,128)} custom-call(s32[192]{0:T(256)} %reshape.10.own_meta, s32[768]{0:T(1024)} %reshape.11.far_meta, f32[8,1056,128]{2,1,0:T(8,128)} %get-tuple-element.7.own_ref, f32[32,1032,128]{2,1,0:T(8,128)} %get-tuple-element.8.far_ref), custom_call_target="tpu_custom_call" | custom-call | tf_op jit(solution)/shard_map/pallas_call | solution.py:309
  (2 shorter events, 0.0 us)

commit v9 on v8

--- a/solution.py
+++ b/solution.py
@@ -12,6 +12,7 @@
 CB_DEV = 16
 META = 8
 MESH = pl.DeviceIdType.MESH
+CHUNKS = 4
 
 
 def pack(tiles, tile_rows, tile_cols, counts, scaling=None):
@@ -30,7 +31,7 @@
     return sets[:, slots * TB : slots * TB + 3, :slots].astype(jnp.int32).reshape(-1)
 
 
-def comm_kernel(n, side, own_half, far_half, own_x, far_x, own_out, far_out, sems, perm_send, perm_recv, z_send, z_recv, f_send, f_recv, p_send, p_recv):
+def comm_kernel(n, side, own_half, n_chunks, own_x, far_x, own_out, far_out, sems, perm_send, perm_recv, z_send, z_recv, f_send, f_recv, p_send, p_recv):
     me = lax.axis_index("cols")
     row = lax.axis_index("rows")
     core = row % 2
@@ -64,16 +65,17 @@
     local_own.start()
 
     far_rows = far_x.shape[0]
-    cut = far_half
-    chunks = (pl.ds(0, cut), pl.ds(cut, far_rows - cut))
-    first_half = (cut // 2) // META * META
-    second_half = ((far_rows - cut) // 2) // META * META
-    halves = (
-        (pl.ds(0, first_half), pl.ds(first_half, cut - first_half)),
-        (pl.ds(cut, second_half), pl.ds(cut + second_half, far_rows - cut - second_half)),
-    )
+    size = (far_rows // n_chunks) // META * META
+    bounds = [h * size for h in range(n_chunks)] + [far_rows]
+    chunks = []
+    halves = []
+    for h in range(n_chunks):
+        low, high = bounds[h], bounds[h + 1]
+        mid = low + ((high - low) // 2) // META * META
+        chunks.append(pl.ds(low, high - low))
+        halves.append((pl.ds(low, mid - low), pl.ds(mid, high - mid)))
     started = []
-    partner_count = [0, 0]
+    partner_count = [0] * n_chunks
     partner_copies = []
 
     def send(src, dst, sem_s, sem_r, peer):
@@ -172,16 +174,15 @@
 
         return [s0, s1, s2, s3, s4, s5]
 
-    lead = far_stages(0)
-    lag = far_stages(1)
-    z_step(0)
-    lead[0]()
-    for tick in range(1, len(lead) + 1):
-        if tick < len(lead):
-            lead[tick]()
-        lag[tick - 1]()
+    streams = [far_stages(h) for h in range(n_chunks)]
+    depth = len(streams[0])
+    ticks = depth + n_chunks - 1
+    for tick in range(ticks):
+        for h in range(n_chunks):
+            if 0 <= tick - h < depth:
+                streams[h][tick - h]()
         z_step(tick)
-    for step in range(len(lead) + 1, n - 1):
+    for step in range(ticks, n - 1):
         z_step(step)
     for way in range(2):
         z_prev[way].wait_recv()
@@ -195,7 +196,7 @@
 def gather_all(own_x, far_x, n, n_far):
     side = 4
     return pl.pallas_call(
-        functools.partial(comm_kernel, n, side, own_x.shape[0] // 2, 512),
+        functools.partial(comm_kernel, n, side, own_x.shape[0] // 2, CHUNKS),
         out_shape=(
             jax.ShapeDtypeStruct((n,) + own_x.shape, own_x.dtype),
             jax.ShapeDtypeStruct((n_far,) + far_x.shape, far_x.dtype),
@@ -204,14 +205,14 @@
         out_specs=(pl.BlockSpec(memory_space=pl.ANY), pl.BlockSpec(memory_space=pl.ANY)),
         scratch_shapes=[
             pltpu.SemaphoreType.DMA((1,)),
-            pltpu.SemaphoreType.DMA((2,)),
-            pltpu.SemaphoreType.DMA((2,)),
+            pltpu.SemaphoreType.DMA((CHUNKS,)),
+            pltpu.SemaphoreType.DMA((CHUNKS,)),
             pltpu.SemaphoreType.DMA((2, n - 1)),
             pltpu.SemaphoreType.DMA((2, n - 1)),
-            pltpu.SemaphoreType.DMA((2, 6, 4)),
-            pltpu.SemaphoreType.DMA((2, 6, 4)),
-            pltpu.SemaphoreType.DMA((2, n_far // 2)),
-            pltpu.SemaphoreType.DMA((2, n_far // 2)),
+            pltpu.SemaphoreType.DMA((CHUNKS, 6, 4)),
+            pltpu.SemaphoreType.DMA((CHUNKS, 6, 4)),
+            pltpu.SemaphoreType.DMA((CHUNKS, n_far // 2)),
+            pltpu.SemaphoreType.DMA((CHUNKS, n_far // 2)),
         ],
         compiler_params=pltpu.CompilerParams(collective_id=0, has_side_effects=True),
     )(own_x, far_x)

time: 167 us -> 165 us (0.988)
  Pallas kernels: 159 us -> 156 us
    pallas_call x1, Pallas kernels: 124 us -> 121 us  [gather_all(): pl.pallas_call(functools.partial(comm_kernel, n, side, own_x.shape[0] //...]
where the time goes in v9:
time: 165 us; the launch traced here: 164 us
  Pallas kernels  156 us (95%)
  other arithmetic  6.36 us (4%)
    pallas_call x1, Pallas kernels, gather_all(): pl.pallas_call(functools.partial(comm_kernel, n, side, own_x.shape[0] //...  121 us
    pallas_call x1, Pallas kernels, per_device(): pl.pallas_call(functools.partial(normal_kernel, slots, far_per, n_cols),...  34.8 us
    concatenate x2, other arithmetic, pack(): return jnp.concatenate(parts, axis=0)  3.94 us

profile of v9, /device:TPU:1, one launch (start us, length us, event | category | flops | bytes accessed | tf_op | source)
XLA Modules:
  0.0 164.3 jit_solution(13238676246438997535)
XLA Ops:
  0.7 0.1 pad.14.clone
  0.7 0.7 add_convert_fusion
  1.5 0.1 pad.11.clone
  1.6 1.9 %pad_maximum_fusion.far_x = f32[1032,128]{1,0:T(8,128)} fusion(f32[8,128]{1,0:T(8,128)S(1)} %pad.5, f32[1024,128]{1,0:T(8,128)} %bitcast.6), kind=kLoop, calls=%fused_computation.1 | loop fusion | flops 132096 | bytes 1056768 | tf_op jit(solution)/shard_map/concatenate | solution.py:27
  3.4 2.1 %maximum_maximum_fusion.own_x = f32[1056,128]{1,0:T(8,128)} fusion(f32[16,128]{1,0:T(8,128)} %bitcast.8, f32[8,128]{1,0:T(8,128)S(1)} %pad.5, f32[1024,128]{1,0:T(8,128)} %bitcast.7, f32[1056]{0:T(1024)S(1)} %pad.11.clone), kind=kLoop, calls=%fused_computation | loop fusion | flops 405504 | bytes 1081472 | tf_op jit(solution)/shard_map/concatenate | solution.py:27
  5.5 121.0 %shard_map.55 = (f32[8,1056,128]{2,1,0:T(8,128)}, f32[32,1032,128]{2,1,0:T(8,128)}) custom-call(f32[1056,128]{1,0:T(8,128)} %maximum_maximum_fusion.own_x, f32[1032,128]{1,0:T(8,128)} %pad_maximum_fusion.far_x), custom_call_target="tpu_custom_call" | custom-call | tf_op jit(solution)/shard_map/pallas_call | solution.py:198
  126.5 0.8 slice_convert_fusion.1
  127.3 0.6 reshape.10.own_meta
  127.9 0.9 slice_convert_fusion
  128.8 0.7 reshape.11.far_meta
  129.5 34.8 %shard_map.56 = f32[256,1024]{1,0:T(8,128)} custom-call(s32[192]{0:T(256)} %reshape.10.own_meta, s32[768]{0:T(1024)} %reshape.11.far_meta, f32[8,1056,128]{2,1,0:T(8,128)} %get-tuple-element.7.own_ref, f32[32,1032,128]{2,1,0:T(8,128)} %get-tuple-element.8.far_ref), custom_call_target="tpu_custom_call" | custom-call | tf_op jit(solution)/shard_map/pallas_call | solution.py:310
  (2 shorter events, 0.0 us)

commit v10 on v9

--- a/solution.py
+++ b/solution.py
@@ -12,7 +12,7 @@
 CB_DEV = 16
 META = 8
 MESH = pl.DeviceIdType.MESH
-CHUNKS = 4
+CHUNKS = 8
 
 
 def pack(tiles, tile_rows, tile_cols, counts, scaling=None):

time: 165 us -> 175 us (1.061)
  Pallas kernels: 156 us -> 166 us
    pallas_call x1, Pallas kernels: 121 us -> 132 us  [gather_all(): pl.pallas_call(functools.partial(comm_kernel, n, side, own_x.shape[0] //...]
where the time goes in v10:
time: 175 us
  Pallas kernels  166 us (95%)
  other arithmetic  6.36 us (4%)
    pallas_call x1, Pallas kernels, gather_all(): pl.pallas_call(functools.partial(comm_kernel, n, side, own_x.shape[0] //...  132 us
    pallas_call x1, Pallas kernels, per_device(): pl.pallas_call(functools.partial(normal_kernel, slots, far_per, n_cols),...  34.8 us
    concatenate x2, other arithmetic, pack(): return jnp.concatenate(parts, axis=0)  3.94 us

profile of v10, /device:TPU:1, one launch (start us, length us, event | category | flops | bytes accessed | tf_op | source)
XLA Modules:
  0.0 174.8 jit_solution(3104290457550903632)
XLA Ops:
  0.7 0.1 pad.14.clone
  0.7 0.7 add_convert_fusion
  1.5 0.1 pad.11.clone
  1.6 1.9 %pad_maximum_fusion.far_x = f32[1032,128]{1,0:T(8,128)} fusion(f32[8,128]{1,0:T(8,128)S(1)} %pad.5, f32[1024,128]{1,0:T(8,128)} %bitcast.6), kind=kLoop, calls=%fused_computation.1 | loop fusion | flops 132096 | bytes 1056768 | tf_op jit(solution)/shard_map/concatenate | solution.py:27
  3.4 2.1 %maximum_maximum_fusion.own_x = f32[1056,128]{1,0:T(8,128)} fusion(f32[16,128]{1,0:T(8,128)} %bitcast.8, f32[8,128]{1,0:T(8,128)S(1)} %pad.5, f32[1024,128]{1,0:T(8,128)} %bitcast.7, f32[1056]{0:T(1024)S(1)} %pad.11.clone), kind=kLoop, calls=%fused_computation | loop fusion | flops 405504 | bytes 1081472 | tf_op jit(solution)/shard_map/concatenate | solution.py:27
  5.5 131.5 %shard_map.55 = (f32[8,1056,128]{2,1,0:T(8,128)}, f32[32,1032,128]{2,1,0:T(8,128)}) custom-call(f32[1056,128]{1,0:T(8,128)} %maximum_maximum_fusion.own_x, f32[1032,128]{1,0:T(8,128)} %pad_maximum_fusion.far_x), custom_call_target="tpu_custom_call" | custom-call | tf_op jit(solution)/shard_map/pallas_call | solution.py:198
  137.0 0.8 slice_convert_fusion.1
  137.8 0.6 reshape.10.own_meta
  138.4 0.9 slice_convert_fusion
  139.3 0.7 reshape.11.far_meta
  140.0 34.8 %shard_map.56 = f32[256,1024]{1,0:T(8,128)} custom-call(s32[192]{0:T(256)} %reshape.10.own_meta, s32[768]{0:T(1024)} %reshape.11.far_meta, f32[8,1056,128]{2,1,0:T(8,128)} %get-tuple-element.7.own_ref, f32[32,1032,128]{2,1,0:T(8,128)} %get-tuple-element.8.far_ref), custom_call_target="tpu_custom_call" | custom-call | tf_op jit(solution)/shard_map/pallas_call | solution.py:310
  (2 shorter events, 0.0 us)

commit v11 on v10

--- a/solution.py
+++ b/solution.py
@@ -12,7 +12,7 @@
 CB_DEV = 16
 META = 8
 MESH = pl.DeviceIdType.MESH
-CHUNKS = 8
+CHUNKS = 3
 
 
 def pack(tiles, tile_rows, tile_cols, counts, scaling=None):

time: 175 us -> 163 us (0.931)
  Pallas kernels: 166 us -> 155 us
    pallas_call x1, Pallas kernels: 132 us -> 120 us  [gather_all(): pl.pallas_call(functools.partial(comm_kernel, n, side, own_x.shape[0] //...]
where the time goes in v11:
time: 163 us
  Pallas kernels  155 us (95%)
  other arithmetic  6.36 us (4%)
    pallas_call x1, Pallas kernels, gather_all(): pl.pallas_call(functools.partial(comm_kernel, n, side, own_x.shape[0] //...  120 us
    pallas_call x1, Pallas kernels, per_device(): pl.pallas_call(functools.partial(normal_kernel, slots, far_per, n_cols),...  34.8 us
    concatenate x2, other arithmetic, pack(): return jnp.concatenate(parts, axis=0)  3.94 us

profile of v11, /device:TPU:1, one launch (start us, length us, event | category | flops | bytes accessed | tf_op | source)
XLA Modules:
  0.0 163.1 jit_solution(1984875354085213118)
XLA Ops:
  0.7 0.1 pad.14.clone
  0.7 0.7 add_convert_fusion
  1.5 0.1 pad.11.clone
  1.6 1.9 %pad_maximum_fusion.far_x = f32[1032,128]{1,0:T(8,128)} fusion(f32[8,128]{1,0:T(8,128)S(1)} %pad.5, f32[1024,128]{1,0:T(8,128)} %bitcast.6), kind=kLoop, calls=%fused_computation.1 | loop fusion | flops 132096 | bytes 1056768 | tf_op jit(solution)/shard_map/concatenate | solution.py:27
  3.4 2.1 %maximum_maximum_fusion.own_x = f32[1056,128]{1,0:T(8,128)} fusion(f32[16,128]{1,0:T(8,128)} %bitcast.8, f32[8,128]{1,0:T(8,128)S(1)} %pad.5, f32[1024,128]{1,0:T(8,128)} %bitcast.7, f32[1056]{0:T(1024)S(1)} %pad.11.clone), kind=kLoop, calls=%fused_computation | loop fusion | flops 405504 | bytes 1081472 | tf_op jit(solution)/shard_map/concatenate | solution.py:27
  5.5 119.8 %shard_map.55 = (f32[8,1056,128]{2,1,0:T(8,128)}, f32[32,1032,128]{2,1,0:T(8,128)}) custom-call(f32[1056,128]{1,0:T(8,128)} %maximum_maximum_fusion.own_x, f32[1032,128]{1,0:T(8,128)} %pad_maximum_fusion.far_x), custom_call_target="tpu_custom_call" | custom-call | tf_op jit(solution)/shard_map/pallas_call | solution.py:198
  125.3 0.8 slice_convert_fusion.1
  126.0 0.6 reshape.10.own_meta
  126.7 0.9 slice_convert_fusion
  127.6 0.7 reshape.11.far_meta
  128.3 34.8 %shard_map.56 = f32[256,1024]{1,0:T(8,128)} custom-call(s32[192]{0:T(256)} %reshape.10.own_meta, s32[768]{0:T(1024)} %reshape.11.far_meta, f32[8,1056,128]{2,1,0:T(8,128)} %get-tuple-element.7.own_ref, f32[32,1032,128]{2,1,0:T(8,128)} %get-tuple-element.8.far_ref), custom_call_target="tpu_custom_call" | custom-call | tf_op jit(solution)/shard_map/pallas_call | solution.py:310
  (2 shorter events, 0.0 us)

commit v12 on v11

--- a/solution.py
+++ b/solution.py
@@ -178,10 +178,10 @@
     depth = len(streams[0])
     ticks = depth + n_chunks - 1
     for tick in range(ticks):
+        z_step(tick)
         for h in range(n_chunks):
             if 0 <= tick - h < depth:
                 streams[h][tick - h]()
-        z_step(tick)
     for step in range(ticks, n - 1):
         z_step(step)
     for way in range(2):

time: 163 us -> 172 us (1.055)
  Pallas kernels: 155 us -> 163 us
    pallas_call x1, Pallas kernels: 120 us -> 128 us  [gather_all(): pl.pallas_call(functools.partial(comm_kernel, n, side, own_x.shape[0] //...]
where the time goes in v12:
time: 172 us
  Pallas kernels  163 us (95%)
  other arithmetic  6.36 us (4%)
    pallas_call x1, Pallas kernels, gather_all(): pl.pallas_call(functools.partial(comm_kernel, n, side, own_x.shape[0] //...  128 us
    pallas_call x1, Pallas kernels, per_device(): pl.pallas_call(functools.partial(normal_kernel, slots, far_per, n_cols),...  35.2 us
    concatenate x2, other arithmetic, pack(): return jnp.concatenate(parts, axis=0)  3.94 us

profile of v12, /device:TPU:1, one launch (start us, length us, event | category | flops | bytes accessed | tf_op | source)
XLA Modules:
  0.0 171.7 jit_solution(9080083747073506051)
XLA Ops:
  0.7 0.1 pad.14.clone
  0.7 0.7 add_convert_fusion
  1.5 0.1 pad.11.clone
  1.6 1.9 %pad_maximum_fusion.far_x = f32[1032,128]{1,0:T(8,128)} fusion(f32[8,128]{1,0:T(8,128)S(1)} %pad.5, f32[1024,128]{1,0:T(8,128)} %bitcast.6), kind=kLoop, calls=%fused_computation.1 | loop fusion | flops 132096 | bytes 1056768 | tf_op jit(solution)/shard_map/concatenate | solution.py:27
  3.4 2.1 %maximum_maximum_fusion.own_x = f32[1056,128]{1,0:T(8,128)} fusion(f32[16,128]{1,0:T(8,128)} %bitcast.8, f32[8,128]{1,0:T(8,128)S(1)} %pad.5, f32[1024,128]{1,0:T(8,128)} %bitcast.7, f32[1056]{0:T(1024)S(1)} %pad.11.clone), kind=kLoop, calls=%fused_computation | loop fusion | flops 405504 | bytes 1081472 | tf_op jit(solution)/shard_map/concatenate | solution.py:27
  5.5 128.0 %shard_map.55 = (f32[8,1056,128]{2,1,0:T(8,128)}, f32[32,1032,128]{2,1,0:T(8,128)}) custom-call(f32[1056,128]{1,0:T(8,128)} %maximum_maximum_fusion.own_x, f32[1032,128]{1,0:T(8,128)} %pad_maximum_fusion.far_x), custom_call_target="tpu_custom_call" | custom-call | tf_op jit(solution)/shard_map/pallas_call | solution.py:198
  133.5 0.8 slice_convert_fusion.1
  134.3 0.6 reshape.10.own_meta
  134.9 0.9 slice_convert_fusion
  135.8 0.7 reshape.11.far_meta
  136.5 35.2 %shard_map.56 = f32[256,1024]{1,0:T(8,128)} custom-call(s32[192]{0:T(256)} %reshape.10.own_meta, s32[768]{0:T(1024)} %reshape.11.far_meta, f32[8,1056,128]{2,1,0:T(8,128)} %get-tuple-element.7.own_ref, f32[32,1032,128]{2,1,0:T(8,128)} %get-tuple-element.8.far_ref), custom_call_target="tpu_custom_call" | custom-call | tf_op jit(solution)/shard_map/pallas_call | solution.py:310
  (2 shorter events, 0.0 us)

commit v13 on v12

--- a/solution.py
+++ b/solution.py
@@ -178,11 +178,12 @@
     depth = len(streams[0])
     ticks = depth + n_chunks - 1
     for tick in range(ticks):
-        z_step(tick)
         for h in range(n_chunks):
             if 0 <= tick - h < depth:
                 streams[h][tick - h]()
-    for step in range(ticks, n - 1):
+        if tick >= 1:
+            z_step(tick - 1)
+    for step in range(ticks - 1, n - 1):
         z_step(step)
     for way in range(2):
         z_prev[way].wait_recv()

time: 172 us -> 166 us (0.965); the launches traced: 172 us -> 163 us
  Pallas kernels: 163 us -> 155 us
    pallas_call x1, Pallas kernels: 128 us -> 119 us  [gather_all(): pl.pallas_call(functools.partial(comm_kernel, n, side, own_x.shape[0] //...]
where the time goes in v13:
time: 166 us; the launch traced here: 163 us
  Pallas kernels  155 us (93%)
  other arithmetic  6.36 us (4%)
    pallas_call x1, Pallas kernels, gather_all(): pl.pallas_call(functools.partial(comm_kernel, n, side, own_x.shape[0] //...  119 us
    pallas_call x1, Pallas kernels, per_device(): pl.pallas_call(functools.partial(normal_kernel, slots, far_per, n_cols),...  35.3 us
    concatenate x2, other arithmetic, pack(): return jnp.concatenate(parts, axis=0)  3.94 us

profile of v13, /device:TPU:1, one launch (start us, length us, event | category | flops | bytes accessed | tf_op | source)
XLA Modules:
  0.0 163.2 jit_solution(5639016641137645534)
XLA Ops:
  0.7 0.1 pad.14.clone
  0.7 0.7 add_convert_fusion
  1.5 0.1 pad.11.clone
  1.6 1.9 %pad_maximum_fusion.far_x = f32[1032,128]{1,0:T(8,128)} fusion(f32[8,128]{1,0:T(8,128)S(1)} %pad.5, f32[1024,128]{1,0:T(8,128)} %bitcast.6), kind=kLoop, calls=%fused_computation.1 | loop fusion | flops 132096 | bytes 1056768 | tf_op jit(solution)/shard_map/concatenate | solution.py:27
  3.4 2.1 %maximum_maximum_fusion.own_x = f32[1056,128]{1,0:T(8,128)} fusion(f32[16,128]{1,0:T(8,128)} %bitcast.8, f32[8,128]{1,0:T(8,128)S(1)} %pad.5, f32[1024,128]{1,0:T(8,128)} %bitcast.7, f32[1056]{0:T(1024)S(1)} %pad.11.clone), kind=kLoop, calls=%fused_computation | loop fusion | flops 405504 | bytes 1081472 | tf_op jit(solution)/shard_map/concatenate | solution.py:27
  5.5 119.3 %shard_map.55 = (f32[8,1056,128]{2,1,0:T(8,128)}, f32[32,1032,128]{2,1,0:T(8,128)}) custom-call(f32[1056,128]{1,0:T(8,128)} %maximum_maximum_fusion.own_x, f32[1032,128]{1,0:T(8,128)} %pad_maximum_fusion.far_x), custom_call_target="tpu_custom_call" | custom-call | tf_op jit(solution)/shard_map/pallas_call | solution.py:199
  124.8 0.8 slice_convert_fusion.1
  125.6 0.6 reshape.10.own_meta
  126.2 0.9 slice_convert_fusion
  127.1 0.7 reshape.11.far_meta
  127.8 35.3 %shard_map.56 = f32[256,1024]{1,0:T(8,128)} custom-call(s32[192]{0:T(256)} %reshape.10.own_meta, s32[768]{0:T(1024)} %reshape.11.far_meta, f32[8,1056,128]{2,1,0:T(8,128)} %get-tuple-element.7.own_ref, f32[32,1032,128]{2,1,0:T(8,128)} %get-tuple-element.8.far_ref), custom_call_target="tpu_custom_call" | custom-call | tf_op jit(solution)/shard_map/pallas_call | solution.py:311
  (2 shorter events, 0.0 us)

commit v14 on v11

--- a/solution.py
+++ b/solution.py
@@ -12,7 +12,7 @@
 CB_DEV = 16
 META = 8
 MESH = pl.DeviceIdType.MESH
-CHUNKS = 3
+CHUNKS = 5
 
 
 def pack(tiles, tile_rows, tile_cols, counts, scaling=None):

time: 163 us -> 167 us (1.025)
  Pallas kernels: 155 us -> 158 us
    pallas_call x1, Pallas kernels: 120 us -> 123 us  [gather_all(): pl.pallas_call(functools.partial(comm_kernel, n, side, own_x.shape[0] //...]
where the time goes in v14:
time: 167 us
  Pallas kernels  158 us (95%)
  other arithmetic  6.36 us (4%)
    pallas_call x1, Pallas kernels, gather_all(): pl.pallas_call(functools.partial(comm_kernel, n, side, own_x.shape[0] //...  123 us
    pallas_call x1, Pallas kernels, per_device(): pl.pallas_call(functools.partial(normal_kernel, slots, far_per, n_cols),...  34.8 us
    concatenate x2, other arithmetic, pack(): return jnp.concatenate(parts, axis=0)  3.94 us

profile of v14, /device:TPU:1, one launch (start us, length us, event | category | flops | bytes accessed | tf_op | source)
XLA Modules:
  0.0 166.6 jit_solution(17799937781584987338)
XLA Ops:
  0.7 0.1 pad.14.clone
  0.7 0.7 add_convert_fusion
  1.5 0.1 pad.11.clone
  1.6 1.9 %pad_maximum_fusion.far_x = f32[1032,128]{1,0:T(8,128)} fusion(f32[8,128]{1,0:T(8,128)S(1)} %pad.5, f32[1024,128]{1,0:T(8,128)} %bitcast.6), kind=kLoop, calls=%fused_computation.1 | loop fusion | flops 132096 | bytes 1056768 | tf_op jit(solution)/shard_map/concatenate | solution.py:27
  3.4 2.1 %maximum_maximum_fusion.own_x = f32[1056,128]{1,0:T(8,128)} fusion(f32[16,128]{1,0:T(8,128)} %bitcast.8, f32[8,128]{1,0:T(8,128)S(1)} %pad.5, f32[1024,128]{1,0:T(8,128)} %bitcast.7, f32[1056]{0:T(1024)S(1)} %pad.11.clone), kind=kLoop, calls=%fused_computation | loop fusion | flops 405504 | bytes 1081472 | tf_op jit(solution)/shard_map/concatenate | solution.py:27
  5.5 123.3 %shard_map.55 = (f32[8,1056,128]{2,1,0:T(8,128)}, f32[32,1032,128]{2,1,0:T(8,128)}) custom-call(f32[1056,128]{1,0:T(8,128)} %maximum_maximum_fusion.own_x, f32[1032,128]{1,0:T(8,128)} %pad_maximum_fusion.far_x), custom_call_target="tpu_custom_call" | custom-call | tf_op jit(solution)/shard_map/pallas_call | solution.py:198
  128.8 0.8 slice_convert_fusion.1
  129.6 0.6 reshape.10.own_meta
  130.3 0.9 slice_convert_fusion
  131.2 0.7 reshape.11.far_meta
  131.9 34.8 %shard_map.56 = f32[256,1024]{1,0:T(8,128)} custom-call(s32[192]{0:T(256)} %reshape.10.own_meta, s32[768]{0:T(1024)} %reshape.11.far_meta, f32[8,1056,128]{2,1,0:T(8,128)} %get-tuple-element.7.own_ref, f32[32,1032,128]{2,1,0:T(8,128)} %get-tuple-element.8.far_ref), custom_call_target="tpu_custom_call" | custom-call | tf_op jit(solution)/shard_map/pallas_call | solution.py:310
  (2 shorter events, 0.0 us)
